TPU v7x, 32 devices: a whole 2x2x4 slice. The times are simulated.
32 devices in a mesh: gy: 8 (over y, x, core), gz: 4 (over z).
Axes of the slice: x: 2, y: 2, z: 4, core: 2. Of those that a mesh axis runs over, the one named last changes fastest.
Arguments:
- magnetic: float32 [3, 192, 32, 256], P(None, 'gy', 'gz'), may hold values from -6 to 6
- velocity: float32 [3, 192, 32, 256], P(None, 'gy', 'gz'), may hold values from -6 to 6
- diffusivity: float32 [192, 32, 256], P('gy', 'gz'), may hold values from 0.5 to 2
- material: int32 [192, 32, 256], P('gy', 'gz'), may hold values 0 or 1
- plane_rate: float32 [32], P('gz'), may hold values from 0.5 to 2000
- cotangent: float32 [3, 192, 32, 256], P(None, 'gy', 'gz'), may hold values from -6 to 6
Outputs:
- new_field: float32 [3, 192, 32, 256], P(None, 'gy', 'gz')
- adjoint_field: float32 [3, 192, 32, 256], P(None, 'gy', 'gz')
Inputs may be any that keep to these rules, and one draw needn't show every extreme that they name: `material`: 1 marks impeller iron.
All inputs are finite; a program needn't handle non-finite values. No bound on the sum of `material` on one device may be relied on, other than what follows from the above.
Results may differ from a plain program's by a relative error of at most 0.000098.
Values sent between devices are 32-bit elements; how exact they have to be, the bound alone decides.
A program may use at most 64 MiB of HBM per device.

v0:
```python
import jax
import jax.numpy as jnp
from jax import lax
from jax.sharding import PartitionSpec as P

step_size = 0.1
iron_factor = 0.2


def extended(cells, sides, width):
    for axis, dim in sides:
        count = lax.axis_size(axis)
        ends = count - 1
        head = lax.slice_in_dim(cells, 0, width, axis=dim)
        tail = lax.slice_in_dim(cells, cells.shape[dim] - width, cells.shape[dim], axis=dim)
        cells = jnp.concatenate(
            [
                lax.ppermute(tail, axis, [(i, (i + 1) % count) for i in range(ends)]),
                cells,
                lax.ppermute(head, axis, [((i + 1) % count, i) for i in range(ends)]),
            ],
            axis=dim,
        )
    return cells


def slope_y(vector):
    return 0.5 * (vector[:, 2:, 1:-1] - vector[:, :-2, 1:-1])


def slope_z(vector):
    return 0.5 * (vector[:, 1:-1, 2:] - vector[:, 1:-1, :-2])


def slope_x(vector):
    inner = vector[:, 1:-1, 1:-1]
    padded = jnp.pad(inner, ((0, 0), (0, 0), (0, 0), (1, 1)))
    return 0.5 * (padded[..., 2:] - padded[..., :-2])


def curl_of(vector):
    along_y = slope_y(vector)
    along_z = slope_z(vector)
    along_x = slope_x(vector)
    return jnp.stack([along_y[2] - along_z[1], along_z[0] - along_x[2], along_x[1] - along_y[0]])


def induction(padded, coefficients):
    inner = padded[:, 1:-1, 1:-1]
    speed = coefficients[:3]
    spread = coefficients[3]
    crossed = jnp.stack(
        [
            speed[1] * inner[2] - speed[2] * inner[1],
            speed[2] * inner[0] - speed[0] * inner[2],
            speed[0] * inner[1] - speed[1] * inner[0],
        ]
    )
    return curl_of(crossed - spread[None] * curl_of(padded))


def solve_tables(line_length, columns, cells_x, plane_rate):
    planes = plane_rate.shape[0]
    flat_index = lax.axis_index("gy") * columns + lax.iota(jnp.int32, columns)
    plane_index = flat_index // cells_x
    onehot = (plane_index[None, :] == lax.iota(jnp.int32, planes)[:, None]).astype(jnp.float32)
    rate_col = jnp.dot(plane_rate, onehot, precision=lax.Precision.HIGHEST)
    mode_index = lax.iota(jnp.int32, line_length) + 1
    product = mode_index[:, None] * mode_index[None, :] % (2 * (line_length + 1))
    sine_table = jnp.sqrt(2.0 / (line_length + 1)) * jnp.sin(
        jnp.pi * product.astype(jnp.float32) / (line_length + 1)
    )
    half_sines = jnp.sin(0.5 * jnp.pi * mode_index.astype(jnp.float32) / (line_length + 1))
    factor = 1.0 / (1.0 + 4.0 * rate_col[None, :] * (half_sines * half_sines)[:, None])
    return (sine_table, factor)


def line_solve(line_data, sine_table, factor):
    flat = line_data[:, :, 0, :]
    spectral = (
        jnp.einsum("ky,cyl->ckl", sine_table, flat, precision=lax.Precision.HIGHEST) * factor[None]
    )
    solved = jnp.einsum("ky,cyl->ckl", sine_table, spectral, precision=lax.Precision.HIGHEST)
    return solved[:, :, None, :]


def local(magnetic, velocity, diffusivity, material, plane_rate, cotangent):
    cells_y = magnetic.shape[1]
    cells_z = magnetic.shape[2]
    cells_x = magnetic.shape[3]
    groups = lax.axis_size("gy")
    columns = cells_z * cells_x // groups
    sine_table, factor = solve_tables(cells_y * groups, columns, cells_x, plane_rate)
    spread = diffusivity * (1.0 - (1.0 - iron_factor) * material.astype(jnp.float32))
    coefficients = jnp.concatenate([velocity, spread[None]], axis=0)

    def to_lines(block_data):
        return block_data.reshape(block_data.shape[0], cells_y, groups, columns)

    def to_cells(block_data):
        return block_data.reshape(block_data.shape[0], cells_y, cells_z, cells_x)

    rims_coef_pad = extended(coefficients, (("gy", 1), ("gz", 2)), 3)
    field_pad = extended(magnetic, (("gy", 1), ("gz", 2)), 2)
    advanced = magnetic + step_size * induction(field_pad, rims_coef_pad[:, 2:-2, 2:-2])
    advanced, coef_pad = (advanced, rims_coef_pad)
    solved_field = lax.all_to_all(
        line_solve(
            lax.all_to_all(to_lines(advanced), "gy", split_axis=2, concat_axis=1, tiled=True),
            sine_table,
            factor,
        ),
        "gy",
        split_axis=1,
        concat_axis=2,
        tiled=True,
    )
    solved_adjoint = lax.all_to_all(
        line_solve(
            lax.all_to_all(to_lines(cotangent), "gy", split_axis=2, concat_axis=1, tiled=True),
            sine_table,
            factor,
        ),
        "gy",
        split_axis=1,
        concat_axis=2,
        tiled=True,
    )
    new_field = to_cells(solved_field)
    relaxed = to_cells(solved_adjoint)
    weight_pad = extended(relaxed, (("gy", 1), ("gz", 2)), 2)
    zero_field = jnp.zeros((3, cells_y + 8, cells_z + 8, cells_x), jnp.float32)
    outcome, pullback = jax.vjp(lambda probe: induction(probe, coef_pad), zero_field)
    pulled = pullback(weight_pad)[0][:, 4:-4, 4:-4]
    adjoint_field = relaxed + step_size * pulled
    return (new_field, adjoint_field)


def solution(mesh):
    in_specs = (
        P(None, "gy", "gz", None),
        P(None, "gy", "gz", None),
        P("gy", "gz", None),
        P("gy", "gz", None),
        P("gz"),
        P(None, "gy", "gz", None),
    )
    out_specs = (P(None, "gy", "gz", None), P(None, "gy", "gz", None))
    return jax.shard_map(local, mesh=mesh, in_specs=in_specs, out_specs=out_specs, check_vma=False)
```

profile of v0, /device:TPU:0, one launch (start us, length us, event | category | flops | bytes accessed | tf_op | source)
XLA Modules:
  0.0 107.7 jit_solution(13163641936337975995)
XLA Ops:
  0.7 1.3 %copy.72 = f32[3,24,8,256]{3,1,2,0:T(8,128)S(1)} copy(f32[3,24,8,256]{3,2,1,0:T(8,128)} %param.6) | data formatting | bytes 1179648 | tf_op args[0]
  2.0 0.7 fusion.82
  2.7 2.4 %collective-permute-start.4 = (f32[3,2,8,256]{3,1,2,0:T(2,128)}, f32[3,2,8,256]{3,1,2,0:T(2,128)S(1)}, u32[]{:S(2)}, u32[]{:S(2)}) collective-permute-start(f32[3,2,8,256]{3,1,2,0:T(2,128)} %get-tuple-element.69), channel_id=1, source_target_pairs={{0,4},{4,8},{8,12},{12,16},{16,20},{20,24},{24,28},{1,5},{5,9},{9,... | collective-permute-start | bytes 147464 | tf_op jit(solution)/shard_map/ppermute | solution.py:18
  5.1 1.4 %collective-permute-start.5 = (f32[3,2,8,256]{3,1,2,0:T(2,128)}, f32[3,2,8,256]{3,1,2,0:T(2,128)}, u32[]{:S(2)}, u32[]{:S(2)}) collective-permute-start(f32[3,2,8,256]{3,1,2,0:T(2,128)} %get-tuple-element.70), channel_id=1, source_target_pairs={{4,0},{8,4},{12,8},{16,12},{20,16},{24,20},{28,24},{5,1},{9,5},{13... | collective-permute-start | bytes 147464 | tf_op jit(solution)/shard_map/ppermute | solution.py:20
  6.9 0.7 pad_maximum_fusion.20
  7.7 5.1 %collective-permute-start = (f32[4,3,8,256]{3,1,2,0:T(4,128)}, f32[4,3,8,256]{3,1,2,0:T(4,128)S(1)}, u32[]{:S(2)}, u32[]{:S(2)}) collective-permute-start(f32[4,3,8,256]{3,1,2,0:T(4,128)} %get-tuple-element.58), channel_id=1, source_target_pairs={{0,4},{4,8},{8,12},{12,16},{16,20},{20,24},{24,28},{1,5},{5,9},{9,... | collective-permute-start | bytes 294920 | tf_op jit(solution)/shard_map/ppermute | solution.py:18
  12.8 1.3 %collective-permute-start.1 = (f32[4,3,8,256]{3,1,2,0:T(4,128)}, f32[4,3,8,256]{3,1,2,0:T(4,128)S(1)}, u32[]{:S(2)}, u32[]{:S(2)}) collective-permute-start(f32[4,3,8,256]{3,1,2,0:T(4,128)} %get-tuple-element.59), channel_id=1, source_target_pairs={{4,0},{8,4},{12,8},{16,12},{20,16},{24,20},{28,24},{5,1},{9,5},{13... | collective-permute-start | bytes 294920 | tf_op jit(solution)/shard_map/ppermute | solution.py:20
  14.1 1.0 copy.77
  15.1 7.1 %all-to-all-start.2 = ((f32[3,24,8,256]{3,1,0,2:T(8,128)}), f32[3,24,8,256]{3,1,0,2:T(8,128)S(1)}, u32[]{:S(2)}, u32[]{:S(2)}) async-start(f32[3,24,8,256]{3,1,0,2:T(8,128)} %copy.77), calls=%async_computation.2 | async-start | bytes 1179648 | tf_op jit(solution)/shard_map/all_to_all | solution.py:120
  22.5 0.8 pad_maximum_fusion.18
  23.4 3.5 %collective-permute-start.6 = (f32[3,28,2,256]{3,1,2,0:T(8,128)S(1)}, f32[3,28,2,256]{3,1,2,0:T(8,128)S(1)}, u32[]{:S(2)}, u32[]{:S(2)}) collective-permute-start(f32[3,28,2,256]{3,1,2,0:T(8,128)S(1)} %get-tuple-element.62), channel_id=1, source_target_pairs={{0,1},{1,2},{2,3},{4,5},{5,6},{6,7},{8,9},{9,10},{10,11},{12,13},{... | collective-permute-start | bytes 516104 | tf_op jit(solution)/shard_map/ppermute | solution.py:18
  26.9 1.3 %collective-permute-start.7 = (f32[3,28,2,256]{3,1,2,0:T(8,128)S(1)}, f32[3,28,2,256]{3,1,2,0:T(8,128)S(1)}, u32[]{:S(2)}, u32[]{:S(2)}) collective-permute-start(f32[3,28,2,256]{3,1,2,0:T(8,128)S(1)} %get-tuple-element.63), channel_id=1, source_target_pairs={{1,0},{2,1},{3,2},{5,4},{6,5},{7,6},{9,8},{10,9},{11,10},{13,12},{... | collective-permute-start | bytes 516104 | tf_op jit(solution)/shard_map/ppermute | solution.py:20
  28.4 4.6 %collective-permute-start.2 = (f32[4,30,3,256]{3,1,2,0:T(8,128)S(1)}, f32[4,30,3,256]{3,1,2,0:T(8,128)S(1)}, u32[]{:S(2)}, u32[]{:S(2)}) collective-permute-start(f32[4,30,3,256]{3,1,2,0:T(8,128)S(1)} %get-tuple-element.38), channel_id=1, source_target_pairs={{0,1},{1,2},{2,3},{4,5},{5,6},{6,7},{8,9},{9,10},{10,11},{12,13},{... | collective-permute-start | bytes 1105928 | tf_op jit(solution)/shard_map/ppermute | solution.py:18
  32.9 1.3 %collective-permute-start.3 = (f32[4,30,3,256]{3,1,2,0:T(8,128)S(1)}, f32[4,30,3,256]{3,1,2,0:T(8,128)S(1)}, u32[]{:S(2)}, u32[]{:S(2)}) collective-permute-start(f32[4,30,3,256]{3,1,2,0:T(8,128)S(1)} %get-tuple-element.39), channel_id=1, source_target_pairs={{1,0},{2,1},{3,2},{5,4},{6,5},{7,6},{9,8},{10,9},{11,10},{13,12},{... | collective-permute-start | bytes 1105928 | tf_op jit(solution)/shard_map/ppermute | solution.py:20
  34.3 1.6 %collective-permute-done.7 = f32[3,28,2,256]{3,1,2,0:T(8,128)S(1)} collective-permute-done((f32[3,28,2,256]{3,1,2,0:T(8,128)S(1)}, f32[3,28,2,256]{3,1,2,0:T(8,128)S(1)}, u32[]{:S(2)}, u32[]{:S(2)}) %collective-permute-start.7) | collective-permute-done | bytes 172064 | tf_op jit(solution)/shard_map/ppermute | solution.py:20
  35.8 1.0 pad_maximum_fusion.1
  37.1 1.6 %fusion.3 = (f32[3,26,10,256]{3,1,2,0:T(8,128)S(1)}, f32[3,26,10,256]{3,1,2,0:T(8,128)S(1)}) fusion(f32[3,26,10,256]{3,1,2,0:T(8,128)S(1)} %get-tuple-element.36, f32[3,2,8,256]{3,1,2,0:T(2,128)} %collective-permute-done.5, f32[3,24,8,256]{3,1,2,0:T(8,128)S(1)} %copy.72, f32[3,2,8,256]{3,1,2,0:T(2,128)S(1)} %collective-permute-done.4, ...), kind=kLoop, calls=%fused_computation.23 | loop fusion | flops 1996800 | bytes 3428352 | tf_op jit(solution)/shard_map/mul | solution.py:38
  38.9 2.5 %collective-permute-done.2 = f32[4,30,3,256]{3,1,2,0:T(8,128)S(1)} collective-permute-done((f32[4,30,3,256]{3,1,2,0:T(8,128)S(1)}, f32[4,30,3,256]{3,1,2,0:T(8,128)S(1)}, u32[]{:S(2)}, u32[]{:S(2)}) %collective-permute-start.2) | collective-permute-done | bytes 368672 | tf_op jit(solution)/shard_map/ppermute | solution.py:18
  41.4 4.1 %collective-permute-done.3 = f32[4,30,3,256]{3,1,2,0:T(8,128)S(1)} collective-permute-done((f32[4,30,3,256]{3,1,2,0:T(8,128)S(1)}, f32[4,30,3,256]{3,1,2,0:T(8,128)S(1)}, u32[]{:S(2)}, u32[]{:S(2)}) %collective-permute-start.3) | collective-permute-done | bytes 368672 | tf_op jit(solution)/shard_map/ppermute | solution.py:20
  46.3 1.2 %fusion.11 = (f32[3,24,8,256]{3,1,2,0:T(8,128)}, f32[3,24,8,256]{3,1,2,0:T(8,128)S(1)}, f32[3,24,8,256]{3,1,2,0:T(8,128)}) fusion(f32[3,26,10,256]{3,1,2,0:T(8,128)S(1)} %maximum_subtract_fusion), kind=kLoop, calls=%fused_computation.48 | loop fusion | flops 589824 | bytes 4718592 | tf_op jit(solution)/shard_map/mul | solution.py:32
  47.6 1.5 %fusion = f32[3,192,256]{2,1,0:T(8,128)S(1)} fusion(f32[3,192,256]{2,1,0:T(8,128)S(1)} %bitcast.59, f32[192,256]{1,0:T(8,128)S(1)} %add_divide_fusion, s32[192]{0:T(256)S(1)} %iota_add_fusion), kind=kOutput, calls=%fused_computation.12 | convolution fusion | flops 340254720 | bytes 1377024 | tf_op jit(solution)/shard_map/ky,cyl->ckl/dot_general | solution.py:81
  49.1 1.5 %convolution_bitcast_fusion = f32[3,192,1,256]{3,1,0,2:T(8,128)S(1)} fusion(f32[3,192,256]{2,1,0:T(8,128)S(1)} %fusion, s32[192]{0:T(256)S(1)} %iota_add_fusion), kind=kOutput, calls=%fused_computation.10 | convolution fusion | flops 340107264 | bytes 1180416 | tf_op jit(solution)/shard_map/ky,cyl->ckl/dot_general | solution.py:83
  50.6 1.4 %copy.79 = f32[3,192,1,256]{3,2,0,1:T(1,128)} copy(f32[3,192,1,256]{3,1,0,2:T(8,128)S(1)} %convolution_bitcast_fusion) | data formatting | bytes 1179648 | tf_op jit(solution)/shard_map/broadcast_in_dim | solution.py:84
  52.0 4.2 %all-to-all-start.3 = ((f32[3,192,1,256]{3,2,0,1:T(1,128)}), f32[3,192,1,256]{3,2,0,1:T(1,128)}, u32[]{:S(2)}, u32[]{:S(2)}) async-start(f32[3,192,1,256]{3,2,0,1:T(1,128)} %copy.79), calls=%async_computation.3 | async-start | bytes 1179648 | tf_op jit(solution)/shard_map/all_to_all | solution.py:118
  56.6 0.7 copy-done.4
  57.9 0.9 copy.73
  58.7 7.9 %all-to-all-done.3 = f32[3,192,1,256]{3,2,0,1:T(1,128)} async-done(((f32[3,192,1,256]{3,2,0,1:T(1,128)}), f32[3,192,1,256]{3,2,0,1:T(1,128)}, u32[]{:S(2)}, u32[]{:S(2)}) %all-to-all-start.3) | async-done | bytes 589856 | tf_op jit(solution)/shard_map/all_to_all | solution.py:118
  66.7 3.5 %all-to-all-start = ((f32[3,24,8,256]{3,1,0,2:T(8,128)}), f32[3,24,8,256]{3,1,0,2:T(8,128)S(1)}, u32[]{:S(2)}, u32[]{:S(2)}) async-start(f32[3,24,8,256]{3,1,0,2:T(8,128)} %copy.73), calls=%async_computation | async-start | bytes 1179648 | tf_op jit(solution)/shard_map/all_to_all | solution.py:109
  70.2 1.1 %copy.80 = f32[3,192,1,256]{3,1,0,2:T(8,128)S(1)} copy(f32[3,192,1,256]{3,2,0,1:T(1,128)} %all-to-all-done.3) | data formatting | bytes 1179648 | tf_op jit(solution)/shard_map/all_to_all | solution.py:118
  71.3 0.7 fusion.81
  72.0 2.3 %collective-permute-start.8 = (f32[3,2,8,256]{3,1,2,0:T(2,128)}, f32[3,2,8,256]{3,1,2,0:T(2,128)S(1)}, u32[]{:S(2)}, u32[]{:S(2)}) collective-permute-start(f32[3,2,8,256]{3,1,2,0:T(2,128)} %get-tuple-element.64), channel_id=1, source_target_pairs={{0,4},{4,8},{8,12},{12,16},{16,20},{20,24},{24,28},{1,5},{5,9},{9,... | collective-permute-start | bytes 147464 | tf_op jit(solution)/shard_map/ppermute | solution.py:18
  74.3 1.3 %collective-permute-start.9 = (f32[3,2,8,256]{3,1,2,0:T(2,128)}, f32[3,2,8,256]{3,1,2,0:T(2,128)}, u32[]{:S(2)}, u32[]{:S(2)}) collective-permute-start(f32[3,2,8,256]{3,1,2,0:T(2,128)} %get-tuple-element.65), channel_id=1, source_target_pairs={{4,0},{8,4},{12,8},{16,12},{20,16},{24,20},{28,24},{5,1},{9,5},{13... | collective-permute-start | bytes 147464 | tf_op jit(solution)/shard_map/ppermute | solution.py:20
  75.6 4.9 %all-to-all-done = f32[3,24,8,256]{3,1,0,2:T(8,128)S(1)} async-done(((f32[3,24,8,256]{3,1,0,2:T(8,128)}), f32[3,24,8,256]{3,1,0,2:T(8,128)S(1)}, u32[]{:S(2)}, u32[]{:S(2)}) %all-to-all-start) | async-done | bytes 589856 | tf_op jit(solution)/shard_map/all_to_all | solution.py:109
  80.6 1.6 %pad_maximum_fusion.15 = (f32[3,28,2,256]{3,1,2,0:T(8,128)}, f32[3,28,2,256]{3,1,2,0:T(8,128)}) fusion(f32[3,2,8,256]{3,1,2,0:T(2,128)} %collective-permute-done.9, f32[3,24,8,256]{3,1,2,0:T(8,128)S(1)} %bitcast.55, f32[3,2,8,256]{3,1,2,0:T(2,128)S(1)} %collective-permute-done.8), kind=kLoop, calls=%fused_computation.79 | loop fusion | flops 172032 | bytes 1032192 | tf_op jit(solution)/shard_map/slice | solution.py:15
  82.2 4.1 %collective-permute-start.10 = (f32[3,28,2,256]{3,1,2,0:T(8,128)}, f32[3,28,2,256]{3,1,2,0:T(8,128)}, u32[]{:S(2)}, u32[]{:S(2)}) collective-permute-start(f32[3,28,2,256]{3,1,2,0:T(8,128)} %get-tuple-element.60), channel_id=1, source_target_pairs={{0,1},{1,2},{2,3},{4,5},{5,6},{6,7},{8,9},{9,10},{10,11},{12,13},{... | collective-permute-start | bytes 516104 | tf_op jit(solution)/shard_map/ppermute | solution.py:18
  86.3 1.5 %collective-permute-start.11 = (f32[3,28,2,256]{3,1,2,0:T(8,128)}, f32[3,28,2,256]{3,1,2,0:T(8,128)}, u32[]{:S(2)}, u32[]{:S(2)}) collective-permute-start(f32[3,28,2,256]{3,1,2,0:T(8,128)} %get-tuple-element.61), channel_id=1, source_target_pairs={{1,0},{2,1},{3,2},{5,4},{6,5},{7,6},{9,8},{10,9},{11,10},{13,12},{... | collective-permute-start | bytes 516104 | tf_op jit(solution)/shard_map/ppermute | solution.py:20
  87.8 1.5 %fusion.1 = f32[3,192,256]{2,1,0:T(8,128)S(1)} fusion(f32[3,192,256]{2,1,0:T(8,128)S(1)} %bitcast.58, f32[192,256]{1,0:T(8,128)S(1)} %copy-done.3, s32[192]{0:T(256)S(1)} %iota_add_fusion), kind=kOutput, calls=%fused_computation.15 | convolution fusion | flops 340254720 | bytes 1377024 | tf_op jit(solution)/shard_map/ky,cyl->ckl/dot_general | solution.py:81
  89.3 1.5 %convolution_bitcast_fusion.1 = f32[3,192,1,256]{3,1,0,2:T(8,128)S(1)} fusion(f32[3,192,256]{2,1,0:T(8,128)S(1)} %fusion.1, s32[192]{0:T(256)S(1)} %iota_add_fusion), kind=kOutput, calls=%fused_computation.13 | convolution fusion | flops 340107264 | bytes 1180416 | tf_op jit(solution)/shard_map/ky,cyl->ckl/dot_general | solution.py:83
  90.8 1.4 %copy.75 = f32[3,192,1,256]{3,2,0,1:T(1,128)} copy(f32[3,192,1,256]{3,1,0,2:T(8,128)S(1)} %convolution_bitcast_fusion.1) | data formatting | bytes 1179648 | tf_op jit(solution)/shard_map/broadcast_in_dim | solution.py:84
  92.3 4.0 %all-to-all-start.1 = ((f32[3,192,1,256]{3,2,0,1:T(1,128)}), f32[3,192,1,256]{3,2,0,1:T(1,128)S(1)}, u32[]{:S(2)}, u32[]{:S(2)}) async-start(f32[3,192,1,256]{3,2,0,1:T(1,128)} %copy.75), calls=%async_computation.1 | async-start | bytes 1179648 | tf_op jit(solution)/shard_map/all_to_all | solution.py:107
  96.2 1.2 %pad_maximum_fusion.2 = f32[3,28,12,256]{3,1,2,0:T(8,128)S(1)} fusion(f32[3,28,2,256]{3,1,2,0:T(8,128)} %collective-permute-done.11, f32[3,2,8,256]{3,1,2,0:T(2,128)} %collective-permute-done.9, f32[3,24,8,256]{3,1,2,0:T(8,128)S(1)} %bitcast.56, f32[3,2,8,256]{3,1,2,0:T(2,128)S(1)} %collective-permute-done.8, f32[3,28,2,256]{3,1,2,0:T(8,128)} %collective-permute-done.10), kind=kLoop, calls=%fused_computation.18 | loop fusion | flops 1032192 | bytes 2064384 | tf_op jit(solution)/shard_map/concatenate | solution.py:16
  98.0 0.7 pad_add_fusion.3
  99.2 1.0 negate_multiply_fusion
  101.3 0.8 pad_add_fusion
  103.0 0.6 fusion.10
  103.6 1.0 copy.82
  104.6 2.0 %all-to-all-done.1 = f32[3,192,1,256]{3,2,0,1:T(1,128)S(1)} async-done(((f32[3,192,1,256]{3,2,0,1:T(1,128)}), f32[3,192,1,256]{3,2,0,1:T(1,128)S(1)}, u32[]{:S(2)}, u32[]{:S(2)}) %all-to-all-start.1) | async-done | bytes 589856 | tf_op jit(solution)/shard_map/all_to_all | solution.py:107
  106.7 1.0 copy.81
  (63 shorter events, 6.2 us)
Async XLA Ops:
  0.6 21.6 %copy-start = (f32[8]{0:T(128)S(1)}, f32[8]{0:T(128)}, u32[]{:S(2)}) copy-start(f32[8]{0:T(128)} %param.10) | copy-start | bytes 100
  0.6 5.9 %copy-start.6 = (f32[3,24,8,256]{3,2,1,0:T(8,128)S(1)}, f32[3,24,8,256]{3,2,1,0:T(8,128)}, u32[]{:S(2)}) copy-start(f32[3,24,8,256]{3,2,1,0:T(8,128)} %param.7) | copy-start | bytes 1769476
  0.7 6.1 %copy-start.11 = (s32[24,8,256]{2,1,0:T(8,128)S(1)}, s32[24,8,256]{2,1,0:T(8,128)}, u32[]{:S(2)}) copy-start(s32[24,8,256]{2,1,0:T(8,128)} %param.9) | copy-start | bytes 589828
  0.7 6.1 %copy-start.10 = (f32[24,8,256]{2,1,0:T(8,128)S(1)}, f32[24,8,256]{2,1,0:T(8,128)}, u32[]{:S(2)}) copy-start(f32[24,8,256]{2,1,0:T(8,128)} %param.8) | copy-start | bytes 589828
  2.7 19.8 %collective-permute-start.4 = (f32[3,2,8,256]{3,1,2,0:T(2,128)}, f32[3,2,8,256]{3,1,2,0:T(2,128)S(1)}, u32[]{:S(2)}, u32[]{:S(2)}) collective-permute-start(f32[3,2,8,256]{3,1,2,0:T(2,128)} %get-tuple-element.69), channel_id=1, source_target_pairs={{0,4},{4,8},{8,12},{12,16},{16,20},{20,24},{24,28},{1,5},{5,9},{9,... | collective-permute-start | bytes 147464 | tf_op jit(solution)/shard_map/ppermute | solution.py:18
  5.1 9.0 %copy-start.7 = (f32[3,24,8,256]{3,2,1,0:T(8,128)S(1)}, f32[3,24,8,256]{3,2,1,0:T(8,128)}, u32[]{:S(2)}) copy-start(f32[3,24,8,256]{3,2,1,0:T(8,128)} %param.11) | copy-start | bytes 1769476
  5.1 17.4 %collective-permute-start.5 = (f32[3,2,8,256]{3,1,2,0:T(2,128)}, f32[3,2,8,256]{3,1,2,0:T(2,128)}, u32[]{:S(2)}, u32[]{:S(2)}) collective-permute-start(f32[3,2,8,256]{3,1,2,0:T(2,128)} %get-tuple-element.70), channel_id=1, source_target_pairs={{4,0},{8,4},{12,8},{16,12},{20,16},{24,20},{28,24},{5,1},{9,5},{13... | collective-permute-start | bytes 147464 | tf_op jit(solution)/shard_map/ppermute | solution.py:20
  7.7 20.5 %collective-permute-start = (f32[4,3,8,256]{3,1,2,0:T(4,128)}, f32[4,3,8,256]{3,1,2,0:T(4,128)S(1)}, u32[]{:S(2)}, u32[]{:S(2)}) collective-permute-start(f32[4,3,8,256]{3,1,2,0:T(4,128)} %get-tuple-element.58), channel_id=1, source_target_pairs={{0,4},{4,8},{8,12},{12,16},{16,20},{20,24},{24,28},{1,5},{5,9},{9,... | collective-permute-start | bytes 294920 | tf_op jit(solution)/shard_map/ppermute | solution.py:18
  12.8 15.4 %collective-permute-start.1 = (f32[4,3,8,256]{3,1,2,0:T(4,128)}, f32[4,3,8,256]{3,1,2,0:T(4,128)S(1)}, u32[]{:S(2)}, u32[]{:S(2)}) collective-permute-start(f32[4,3,8,256]{3,1,2,0:T(4,128)} %get-tuple-element.59), channel_id=1, source_target_pairs={{4,0},{8,4},{12,8},{16,12},{20,16},{24,20},{28,24},{5,1},{9,5},{13... | collective-permute-start | bytes 294920 | tf_op jit(solution)/shard_map/ppermute | solution.py:20
  15.1 32.4 %all-to-all-start.2 = ((f32[3,24,8,256]{3,1,0,2:T(8,128)}), f32[3,24,8,256]{3,1,0,2:T(8,128)S(1)}, u32[]{:S(2)}, u32[]{:S(2)}) async-start(f32[3,24,8,256]{3,1,0,2:T(8,128)} %copy.77), calls=%async_computation.2 | async-start | bytes 1179648 | tf_op jit(solution)/shard_map/all_to_all | solution.py:120
  22.5 25.1 %copy-start.2 = (f32[192,256]{1,0:T(8,128)}, f32[192,256]{1,0:T(8,128)S(1)}, u32[]{:S(2)}) copy-start(f32[192,256]{1,0:T(8,128)S(1)} %add_divide_fusion) | copy-start | bytes 589828
  23.4 10.9 %collective-permute-start.6 = (f32[3,28,2,256]{3,1,2,0:T(8,128)S(1)}, f32[3,28,2,256]{3,1,2,0:T(8,128)S(1)}, u32[]{:S(2)}, u32[]{:S(2)}) collective-permute-start(f32[3,28,2,256]{3,1,2,0:T(8,128)S(1)} %get-tuple-element.62), channel_id=1, source_target_pairs={{0,1},{1,2},{2,3},{4,5},{5,6},{6,7},{8,9},{9,10},{10,11},{12,13},{... | collective-permute-start | bytes 516104 | tf_op jit(solution)/shard_map/ppermute | solution.py:18
  26.9 8.9 %collective-permute-start.7 = (f32[3,28,2,256]{3,1,2,0:T(8,128)S(1)}, f32[3,28,2,256]{3,1,2,0:T(8,128)S(1)}, u32[]{:S(2)}, u32[]{:S(2)}) collective-permute-start(f32[3,28,2,256]{3,1,2,0:T(8,128)S(1)} %get-tuple-element.63), channel_id=1, source_target_pairs={{1,0},{2,1},{3,2},{5,4},{6,5},{7,6},{9,8},{10,9},{11,10},{13,12},{... | collective-permute-start | bytes 516104 | tf_op jit(solution)/shard_map/ppermute | solution.py:20
  28.2 7.6 %copy-start.8 = (f32[4,3,8,256]{3,1,2,0:T(4,128)}, f32[4,3,8,256]{3,1,2,0:T(4,128)S(1)}, u32[]{:S(2)}) copy-start(f32[4,3,8,256]{3,1,2,0:T(4,128)S(1)} %collective-permute-done.1) | copy-start | bytes 294916
  28.4 13.0 %collective-permute-start.2 = (f32[4,30,3,256]{3,1,2,0:T(8,128)S(1)}, f32[4,30,3,256]{3,1,2,0:T(8,128)S(1)}, u32[]{:S(2)}, u32[]{:S(2)}) collective-permute-start(f32[4,30,3,256]{3,1,2,0:T(8,128)S(1)} %get-tuple-element.38), channel_id=1, source_target_pairs={{0,1},{1,2},{2,3},{4,5},{5,6},{6,7},{8,9},{9,10},{10,11},{12,13},{... | collective-permute-start | bytes 1105928 | tf_op jit(solution)/shard_map/ppermute | solution.py:18
  32.9 12.6 %collective-permute-start.3 = (f32[4,30,3,256]{3,1,2,0:T(8,128)S(1)}, f32[4,30,3,256]{3,1,2,0:T(8,128)S(1)}, u32[]{:S(2)}, u32[]{:S(2)}) collective-permute-start(f32[4,30,3,256]{3,1,2,0:T(8,128)S(1)} %get-tuple-element.39), channel_id=1, source_target_pairs={{1,0},{2,1},{3,2},{5,4},{6,5},{7,6},{9,8},{10,9},{11,10},{13,12},{... | collective-permute-start | bytes 1105928 | tf_op jit(solution)/shard_map/ppermute | solution.py:20
  38.7 6.8 %copy-start.9 = (f32[4,3,8,256]{3,1,2,0:T(4,128)S(1)}, f32[4,3,8,256]{3,1,2,0:T(4,128)}, u32[]{:S(2)}) copy-start(f32[4,3,8,256]{3,1,2,0:T(4,128)} %copy-done.8) | copy-start | bytes 294916
  52.0 14.6 %all-to-all-start.3 = ((f32[3,192,1,256]{3,2,0,1:T(1,128)}), f32[3,192,1,256]{3,2,0,1:T(1,128)}, u32[]{:S(2)}, u32[]{:S(2)}) async-start(f32[3,192,1,256]{3,2,0,1:T(1,128)} %copy.79), calls=%async_computation.3 | async-start | bytes 1179648 | tf_op jit(solution)/shard_map/all_to_all | solution.py:118
  56.2 1.1 copy-start.4
  56.2 1.2 %copy-start.5 = (f32[3,24,8,256]{3,1,2,0:T(8,128)S(1)}, f32[3,24,8,256]{3,1,2,0:T(8,128)}, u32[]{:S(2)}) copy-start(f32[3,24,8,256]{3,1,2,0:T(8,128)} %get-tuple-element.42) | copy-start | bytes 1769476
  56.3 1.4 %copy-start.1 = (f32[3,24,8,256]{3,2,1,0:T(8,128)S(1)}, f32[3,24,8,256]{3,2,1,0:T(8,128)}, u32[]{:S(2)}) copy-start(f32[3,24,8,256]{3,2,1,0:T(8,128)} %param.6) | copy-start | bytes 1769476
  66.7 13.9 %all-to-all-start = ((f32[3,24,8,256]{3,1,0,2:T(8,128)}), f32[3,24,8,256]{3,1,0,2:T(8,128)S(1)}, u32[]{:S(2)}, u32[]{:S(2)}) async-start(f32[3,24,8,256]{3,1,0,2:T(8,128)} %copy.73), calls=%async_computation | async-start | bytes 1179648 | tf_op jit(solution)/shard_map/all_to_all | solution.py:109
  72.0 8.6 %collective-permute-start.8 = (f32[3,2,8,256]{3,1,2,0:T(2,128)}, f32[3,2,8,256]{3,1,2,0:T(2,128)S(1)}, u32[]{:S(2)}, u32[]{:S(2)}) collective-permute-start(f32[3,2,8,256]{3,1,2,0:T(2,128)} %get-tuple-element.64), channel_id=1, source_target_pairs={{0,4},{4,8},{8,12},{12,16},{16,20},{20,24},{24,28},{1,5},{5,9},{9,... | collective-permute-start | bytes 147464 | tf_op jit(solution)/shard_map/ppermute | solution.py:18
  74.3 6.3 %collective-permute-start.9 = (f32[3,2,8,256]{3,1,2,0:T(2,128)}, f32[3,2,8,256]{3,1,2,0:T(2,128)}, u32[]{:S(2)}, u32[]{:S(2)}) collective-permute-start(f32[3,2,8,256]{3,1,2,0:T(2,128)} %get-tuple-element.65), channel_id=1, source_target_pairs={{4,0},{8,4},{12,8},{16,12},{20,16},{24,20},{28,24},{5,1},{9,5},{13... | collective-permute-start | bytes 147464 | tf_op jit(solution)/shard_map/ppermute | solution.py:20
  80.6 7.2 %copy-start.3 = (f32[192,256]{1,0:T(8,128)S(1)}, f32[192,256]{1,0:T(8,128)}, u32[]{:S(2)}) copy-start(f32[192,256]{1,0:T(8,128)} %copy-done.2) | copy-start | bytes 589828
  82.2 14.0 %collective-permute-start.10 = (f32[3,28,2,256]{3,1,2,0:T(8,128)}, f32[3,28,2,256]{3,1,2,0:T(8,128)}, u32[]{:S(2)}, u32[]{:S(2)}) collective-permute-start(f32[3,28,2,256]{3,1,2,0:T(8,128)} %get-tuple-element.60), channel_id=1, source_target_pairs={{0,1},{1,2},{2,3},{4,5},{5,6},{6,7},{8,9},{9,10},{10,11},{12,13},{... | collective-permute-start | bytes 516104 | tf_op jit(solution)/shard_map/ppermute | solution.py:18
  86.3 9.9 %collective-permute-start.11 = (f32[3,28,2,256]{3,1,2,0:T(8,128)}, f32[3,28,2,256]{3,1,2,0:T(8,128)}, u32[]{:S(2)}, u32[]{:S(2)}) collective-permute-start(f32[3,28,2,256]{3,1,2,0:T(8,128)} %get-tuple-element.61), channel_id=1, source_target_pairs={{1,0},{2,1},{3,2},{5,4},{6,5},{7,6},{9,8},{10,9},{11,10},{13,12},{... | collective-permute-start | bytes 516104 | tf_op jit(solution)/shard_map/ppermute | solution.py:20
  92.3 14.4 %all-to-all-start.1 = ((f32[3,192,1,256]{3,2,0,1:T(1,128)}), f32[3,192,1,256]{3,2,0,1:T(1,128)S(1)}, u32[]{:S(2)}, u32[]{:S(2)}) async-start(f32[3,192,1,256]{3,2,0,1:T(1,128)} %copy.75), calls=%async_computation.1 | async-start | bytes 1179648 | tf_op jit(solution)/shard_map/all_to_all | solution.py:107
where the time goes:
time: 109 us; the launch traced here: 108 us
  starting transfers between devices  48.8 us (45%)
  waiting for transfers between devices  23.1 us (21%)
  other arithmetic  16.5 us (15%)
  local copies, waits for them, and re-layouts  11.9 us (11%)
  matrix products  6.11 us (6%)
  between operations  1.24 us (1%)
    ppermute x6, starting transfers between devices, extended(): lax.ppermute(tail, axis, [(i, (i + 1) % count) for i in range(ends)])  22 us
    ppermute x6, starting transfers between devices, extended(): lax.ppermute(head, axis, [((i + 1) % count, i) for i in range(ends)])  8.05 us
    all_to_all x1, waiting for transfers between devices, local(): lax.all_to_all(line_solve(lax.all_to_all(to_lines(cotangent), 'gy', split...  7.92 us
    all_to_all x1, starting transfers between devices, local(): lax.all_to_all(to_lines(cotangent), 'gy', split_axis=2, concat_axis=1, ti...  7.08 us
    ppermute x6, waiting for transfers between devices, extended(): lax.ppermute(head, axis, [((i + 1) % count, i) for i in range(ends)])  5.71 us
    unnamed x29, local copies, waits for them, and re-layouts  5.53 us
    all_to_all x1, waiting for transfers between devices, local(): lax.all_to_all(to_lines(advanced), 'gy', split_axis=2, concat_axis=1, til...  4.92 us
    all_to_all x1, starting transfers between devices, local(): lax.all_to_all(line_solve(lax.all_to_all(to_lines(cotangent), 'gy', split...  4.19 us
  transfers between devices with their start and end apart: 16, of which 6 were waited for; matrix products, arithmetic and copies ran while one was open for 23% of the time, Pallas kernels for 0%

commit v1 on v0

v1 whole, which is shorter than its diff:
```python
import functools
import jax
import jax.numpy as jnp
from jax import lax
from jax.experimental import pallas as pl
from jax.experimental.pallas import tpu as pltpu
from jax.sharding import PartitionSpec as P

step_size = 0.1
iron_factor = 0.2
MESH = pl.DeviceIdType.MESH
Y_PARTS = (0, 2)
Z_PARTS = (0, 1)


def kernel(
    groups, layers, n, mag, vel, dif, mat, rate, cot, new_out, adj_out,
    bE, gE, wE, hE, v, eta, iron, adj, new, zs, zr, ends, m_tab, inv_tab, al_tab, s_tab, den_tab,
    load_sem, out_sem, ys_sem, yr_sem, zs_sem, zr_sem, gs_sem, gr_sem,
):
    me = lax.axis_index("gy")
    lay = lax.axis_index("gz")
    nx = bE.shape[-1]
    nz = bE.shape[-2]

    loads = [
        pltpu.make_async_copy(mag, bE.at[:, pl.ds(1, n)], load_sem.at[0]),
        pltpu.make_async_copy(cot, wE.at[:, pl.ds(1, n)], load_sem.at[1]),
        pltpu.make_async_copy(vel, v, load_sem.at[2]),
        pltpu.make_async_copy(dif, eta, load_sem.at[3]),
        pltpu.make_async_copy(mat, iron, load_sem.at[4]),
    ]
    for load in loads:
        load.start()

    has_left, has_right = me > 0, me < groups - 1
    has_low, has_high = lay > 0, lay < layers - 1

    barrier = pltpu.get_barrier_semaphore()
    for k in range(1, groups):
        pl.semaphore_signal(
            barrier, inc=1, device_id={"gy": lax.rem(me + k, groups), "gz": lay}, device_id_type=MESH
        )

    @pl.when(has_low)
    def _():
        pl.semaphore_signal(barrier, inc=1, device_id={"gy": me, "gz": lay - 1}, device_id_type=MESH)

    @pl.when(has_high)
    def _():
        pl.semaphore_signal(barrier, inc=1, device_id={"gy": me, "gz": lay + 1}, device_id_type=MESH)

    rim = jnp.zeros((nz, nx), jnp.float32)
    for field in (bE, gE, hE):
        for part in Y_PARTS:
            @pl.when(jnp.logical_not(has_left))
            def _():
                field[part, 0] = rim

            @pl.when(jnp.logical_not(has_right))
            def _():
                field[part, n + 1] = rim

    @pl.when(jnp.logical_not(has_low))
    def _():
        zr[:, 0] = jnp.zeros(zr.shape[:1] + zr.shape[2:], jnp.float32)

    @pl.when(jnp.logical_not(has_high))
    def _():
        zr[:, 1] = jnp.zeros(zr.shape[:1] + zr.shape[2:], jnp.float32)

    sub = lax.broadcasted_iota(jnp.int32, (nz, nx), 0)
    lane = lax.broadcasted_iota(jnp.int32, (nz, nx), 1)
    square = (
        lax.broadcasted_iota(jnp.int32, (nz, nz), 0) == lax.broadcasted_iota(jnp.int32, (nz, nz), 1)
    )
    r = jnp.sum(jnp.where(square, jnp.broadcast_to(rate[...], (nz, nz)), 0.0), axis=1, keepdims=True)
    r = jnp.broadcast_to(r, (nz, nx))

    def pivot(k, p):
        inv = 1.0 / (r + p)
        m = r * inv
        m_tab[k] = m
        inv_tab[k] = inv
        return 1.0 + m * p

    lax.fori_loop(0, n, pivot, 1.0 + r)

    def response(k, above):
        here = m_tab[n - 1 - k] * above
        al_tab[k] = here
        return here

    cc = lax.fori_loop(0, n, response, jnp.ones((nz, nx), jnp.float32))
    aa = m_tab[n - 1]

    def reach(k, s):
        s_tab[k] = s
        den = cc / (1.0 - s * aa)
        den_tab[k] = den
        return aa + cc * s * den

    lax.fori_loop(0, groups, reach, jnp.zeros((nz, nx), jnp.float32))

    def local_solve(field, offset, slot):
        def down(k, held):
            m = m_tab[jnp.maximum(k - 1, 0)]
            rows = tuple(field[c, offset + k] + m * held[c] for c in range(3))
            for c in range(3):
                field[c, offset + k] = rows[c]
            return rows

        zero = jnp.zeros((nz, nx), jnp.float32)
        lax.fori_loop(0, n, down, (zero, zero, zero), unroll=True)

        def up(step, held):
            k = n - 1 - step
            m, inv = m_tab[k], inv_tab[k]
            rows = tuple(field[c, offset + k] * inv + m * held[c] for c in range(3))
            for c in range(3):
                field[c, offset + k] = rows[c]
            return rows

        lax.fori_loop(0, n, up, (zero, zero, zero), unroll=True)
        for c in range(3):
            ends[slot, me, 0, c] = field[c, offset]
            ends[slot, me, 1, c] = field[c, offset + n - 1]

    def gather(slot):
        return [
            pltpu.make_async_remote_copy(
                src_ref=ends.at[slot, me], dst_ref=ends.at[slot, me],
                send_sem=gs_sem.at[slot, k], recv_sem=gr_sem.at[slot, k],
                device_id={"gy": lax.rem(me + k, groups), "gz": lay}, device_id_type=MESH,
            )
            for k in range(1, groups)
        ]

    def gather_wait(slot):
        for k in range(1, groups):
            src = lax.rem(me + groups - k, groups)
            pltpu.make_async_remote_copy(
                src_ref=ends.at[slot, src], dst_ref=ends.at[slot, src],
                send_sem=gs_sem.at[slot, k], recv_sem=gr_sem.at[slot, k],
                device_id={"gy": src, "gz": lay}, device_id_type=MESH,
            ).wait_recv()

    def interface(slot):
        zero = jnp.zeros((nz, nx), jnp.float32)

        def sweep(k, held):
            low, high, s_low, s_high = held
            s, den = s_tab[k], den_tab[k]
            take_low = k < me
            far = groups - 1 - k
            take_high = far > me
            low = tuple(
                jnp.where(take_low, ends[slot, k, 1, c] + den * (low[c] + s * ends[slot, k, 0, c]), low[c])
                for c in range(3)
            )
            high = tuple(
                jnp.where(take_high, ends[slot, far, 0, c] + den * (high[c] + s * ends[slot, far, 1, c]), high[c])
                for c in range(3)
            )
            after = s_tab[k + 1]
            s_low = jnp.where(take_low, after, s_low)
            s_high = jnp.where(take_high, after, s_high)
            return low, high, s_low, s_high

        zeros = (zero, zero, zero)
        low, high, s_low, s_high = lax.fori_loop(0, groups - 1, sweep, (zeros, zeros, zero, zero))
        left_gap, right_gap = 1.0 - s_low * aa, 1.0 - s_high * aa
        det = 1.0 / (left_gap * right_gap - s_low * s_high * cc * cc)
        lefts, rights = [], []
        for c in range(3):
            x = low[c] + s_low * ends[slot, me, 0, c]
            y = high[c] + s_high * ends[slot, me, 1, c]
            lefts.append((right_gap * x + s_low * cc * y) * det)
            rights.append((left_gap * y + s_high * cc * x) * det)
        return lefts, rights

    def y_copies(field, ex):
        lefts, rights = [], []
        for i, part in enumerate(Y_PARTS):
            lefts.append(pltpu.make_async_remote_copy(
                src_ref=field.at[part, 1], dst_ref=field.at[part, n + 1],
                send_sem=ys_sem.at[ex, 0, i], recv_sem=yr_sem.at[ex, 0, i],
                device_id={"gy": jnp.maximum(me - 1, 0), "gz": lay}, device_id_type=MESH))
            rights.append(pltpu.make_async_remote_copy(
                src_ref=field.at[part, n], dst_ref=field.at[part, 0],
                send_sem=ys_sem.at[ex, 1, i], recv_sem=yr_sem.at[ex, 1, i],
                device_id={"gy": jnp.minimum(me + 1, groups - 1), "gz": lay}, device_id_type=MESH))
        return lefts, rights

    def z_copies(ex):
        low = pltpu.make_async_remote_copy(
            src_ref=zs.at[ex, 0], dst_ref=zr.at[ex, 1],
            send_sem=zs_sem.at[ex, 0], recv_sem=zr_sem.at[ex, 0],
            device_id={"gy": me, "gz": jnp.maximum(lay - 1, 0)}, device_id_type=MESH)
        high = pltpu.make_async_remote_copy(
            src_ref=zs.at[ex, 1], dst_ref=zr.at[ex, 0],
            send_sem=zs_sem.at[ex, 1], recv_sem=zr_sem.at[ex, 1],
            device_id={"gy": me, "gz": jnp.minimum(lay + 1, layers - 1)}, device_id_type=MESH)
        return low, high

    def send_y(field, ex):
        lefts, rights = y_copies(field, ex)

        @pl.when(has_left)
        def _():
            for copy in lefts:
                copy.start()

        @pl.when(has_right)
        def _():
            for copy in rights:
                copy.start()

    def send_z(ex):
        low, high = z_copies(ex)

        @pl.when(has_low)
        def _():
            low.start()

        @pl.when(has_high)
        def _():
            high.start()

    def recv(field, ex):
        low, high = z_copies(ex)
        if field is not None:
            lefts, rights = y_copies(field, ex)

            @pl.when(has_right)
            def _():
                for copy in lefts:
                    copy.wait_recv()

            @pl.when(has_left)
            def _():
                for copy in rights:
                    copy.wait_recv()

        @pl.when(has_high)
        def _():
            low.wait_recv()

        @pl.when(has_low)
        def _():
            high.wait_recv()

    def done_sending(field, ex):
        low, high = z_copies(ex)
        if field is not None:
            lefts, rights = y_copies(field, ex)

            @pl.when(has_left)
            def _():
                for copy in lefts:
                    copy.wait_send()

            @pl.when(has_right)
            def _():
                for copy in rights:
                    copy.wait_send()

        @pl.when(has_low)
        def _():
            low.wait_send()

        @pl.when(has_high)
        def _():
            high.wait_send()

    def stage(ex, y, rows):
        for i in range(2):
            zs[ex, 0, i, pl.ds(y, 1), :] = rows[i][0:1]
            zs[ex, 1, i, pl.ds(y, 1), :] = rows[i][nz - 1:nz]

    def slope_x(f):
        ahead = jnp.where(lane == nx - 1, 0.0, pltpu.roll(f, nx - 1, 1))
        behind = jnp.where(lane == 0, 0.0, pltpu.roll(f, 1, 1))
        return 0.5 * (ahead - behind)

    def slope_z(f, ex, i, y):
        below = jnp.broadcast_to(zr[ex, 0, i, pl.ds(y, 1), :], (nz, nx))
        above = jnp.broadcast_to(zr[ex, 1, i, pl.ds(y, 1), :], (nz, nx))
        ahead = jnp.where(sub == nz - 1, above, pltpu.roll(f, nz - 1, 0))
        behind = jnp.where(sub == 0, below, pltpu.roll(f, 1, 0))
        return 0.5 * (ahead - behind)

    def curl(field, ex, y):
        f = [field[c, y + 1] for c in range(3)]
        dy_x = 0.5 * (field[0, y + 2] - field[0, y])
        dy_z = 0.5 * (field[2, y + 2] - field[2, y])
        return (
            dy_z - slope_z(f[1], ex, 1, y),
            slope_z(f[0], ex, 0, y) - slope_x(f[2]),
            slope_x(f[1]) - dy_x,
        ), f

    def each_row(body, unroll=2):
        def some(step, carry):
            for u in range(unroll):
                body(step * unroll + u)
            return carry

        lax.fori_loop(0, n // unroll, some, 0)

    loads[0].wait()
    each_row(lambda y: stage(0, y, (bE[0, y + 1], bE[1, y + 1])), 4)
    count = groups - 1 + has_low.astype(jnp.int32) + has_high.astype(jnp.int32)
    pl.semaphore_wait(barrier, count)
    send_y(bE, 0)
    send_z(0)

    loads[1].wait()
    local_solve(wE, 1, 0)
    for copy in gather(0):
        copy.start()

    for load in loads[2:]:
        load.wait()
    recv(bE, 0)

    def argument(y):
        spread = eta[y] * (1.0 - (1.0 - iron_factor) * iron[y].astype(jnp.float32))
        eta[y] = spread
        turn, b = curl(bE, 0, y)
        s = [v[c, y] for c in range(3)]
        rows = (
            s[1] * b[2] - s[2] * b[1] - spread * turn[0],
            s[2] * b[0] - s[0] * b[2] - spread * turn[1],
            s[0] * b[1] - s[1] * b[0] - spread * turn[2],
        )
        for c in range(3):
            gE[c, y + 1] = rows[c]
        stage(1, y, rows)

    each_row(argument)
    send_y(gE, 1)
    send_z(1)

    gather_wait(0)
    lefts, rights = interface(0)
    for c in range(3):
        wE[c, 0] = lefts[c]
        wE[c, n + 1] = rights[c]

    def relax(y):
        near, far = al_tab[y], al_tab[n - 1 - y]
        rows = [wE[c, y + 1] + near * wE[c, 0] + far * wE[c, n + 1] for c in range(3)]
        for c in range(3):
            wE[c, y + 1] = rows[c]
        stage(2, y, rows)

    each_row(relax)
    send_z(2)

    recv(gE, 1)

    def advance(y):
        turn, _ = curl(gE, 1, y)
        for c in range(3):
            new[c, y] = bE[c, y + 1] + step_size * turn[c]

    each_row(advance)
    local_solve(new, 0, 1)
    for copy in gather(1):
        copy.start()

    recv(None, 2)

    def pull(y):
        turn, w = curl(wE, 2, y)
        s = [v[c, y] for c in range(3)]
        spread = eta[y]
        adj[0, y] = w[0] + step_size * (turn[1] * s[2] - turn[2] * s[1])
        adj[1, y] = w[1] + step_size * (turn[2] * s[0] - turn[0] * s[2])
        adj[2, y] = w[2] + step_size * (turn[0] * s[1] - turn[1] * s[0])
        rows = [spread * turn[c] for c in range(3)]
        for c in range(3):
            hE[c, y + 1] = rows[c]
        stage(3, y, rows)

    each_row(pull)
    send_y(hE, 3)
    send_z(3)

    gather_wait(1)
    lefts, rights = interface(1)
    for c in range(3):
        gE[c, 0] = lefts[c]
        gE[c, n + 1] = rights[c]

    def finish(y):
        near, far = al_tab[y], al_tab[n - 1 - y]
        for c in range(3):
            new[c, y] = new[c, y] + near * gE[c, 0] + far * gE[c, n + 1]

    each_row(finish)
    new_copy = pltpu.make_async_copy(new, new_out, out_sem.at[0])
    new_copy.start()

    recv(hE, 3)

    def finish_adjoint(y):
        turn, _ = curl(hE, 3, y)
        for c in range(3):
            adj[c, y] = adj[c, y] - step_size * turn[c]

    each_row(finish_adjoint)
    adj_copy = pltpu.make_async_copy(adj, adj_out, out_sem.at[1])
    adj_copy.start()
    done_sending(bE, 0)
    done_sending(gE, 1)
    done_sending(None, 2)
    done_sending(hE, 3)
    for slot in range(2):
        for copy in gather(slot):
            copy.wait_send()
    new_copy.wait()
    adj_copy.wait()


def local(groups, layers, magnetic, velocity, diffusivity, material, plane_rate, cotangent):
    _, n, nz, nx = magnetic.shape
    block = (3, n, nz, nx)
    rimmed = (3, n + 2, nz, nx)
    f32 = jnp.float32
    anywhere = pl.BlockSpec(memory_space=pl.ANY)
    inside = pl.BlockSpec(memory_space=pltpu.VMEM)
    return tuple(pl.pallas_call(
        functools.partial(kernel, groups, layers, n),
        out_shape=[jax.ShapeDtypeStruct(block, f32)] * 2,
        in_specs=[anywhere] * 4 + [inside] + [anywhere],
        out_specs=[anywhere] * 2,
        scratch_shapes=[
            pltpu.VMEM(rimmed, f32),
            pltpu.VMEM(rimmed, f32),
            pltpu.VMEM(rimmed, f32),
            pltpu.VMEM(rimmed, f32),
            pltpu.VMEM(block, f32),
            pltpu.VMEM((n, nz, nx), f32),
            pltpu.VMEM((n, nz, nx), jnp.int32),
            pltpu.VMEM(block, f32),
            pltpu.VMEM(block, f32),
            pltpu.VMEM((4, 2, 2, n, nx), f32),
            pltpu.VMEM((4, 2, 2, n, nx), f32),
            pltpu.VMEM((2, groups, 2, 3, nz, nx), f32),
            pltpu.VMEM((n, nz, nx), f32),
            pltpu.VMEM((n, nz, nx), f32),
            pltpu.VMEM((n, nz, nx), f32),
            pltpu.VMEM((groups, nz, nx), f32),
            pltpu.VMEM((groups, nz, nx), f32),
            pltpu.SemaphoreType.DMA((5,)),
            pltpu.SemaphoreType.DMA((2,)),
            pltpu.SemaphoreType.DMA((4, 2, 2)),
            pltpu.SemaphoreType.DMA((4, 2, 2)),
            pltpu.SemaphoreType.DMA((4, 2)),
            pltpu.SemaphoreType.DMA((4, 2)),
            pltpu.SemaphoreType.DMA((2, groups)),
            pltpu.SemaphoreType.DMA((2, groups)),
        ],
        compiler_params=pltpu.CompilerParams(
            collective_id=0, has_side_effects=True, vmem_limit_bytes=24 * 2**20
        ),
    )(magnetic, velocity, diffusivity, material, plane_rate.reshape(1, nz), cotangent))


def solution(mesh):
    in_specs = (
        P(None, "gy", "gz", None),
        P(None, "gy", "gz", None),
        P("gy", "gz", None),
        P("gy", "gz", None),
        P("gz"),
        P(None, "gy", "gz", None),
    )
    out_specs = (P(None, "gy", "gz", None), P(None, "gy", "gz", None))
    body = functools.partial(local, mesh.shape["gy"], mesh.shape["gz"])
    return jax.shard_map(body, mesh=mesh, in_specs=in_specs, out_specs=out_specs, check_vma=False)
```

time: 109 us -> 29.9 us (0.27)
  starting transfers between devices: 48.8 us -> 0 us
  waiting for transfers between devices: 23.1 us -> 0 us
  Pallas kernels: 0 us -> 21.5 us
  other arithmetic: 16.5 us -> 0 us
  matrix products: 6.11 us -> 0 us
  local copies, waits for them, and re-layouts: 11.9 us -> 7.32 us
    ppermute x12 -> x0, starting transfers between devices: 30.1 us -> none  [the longest x6 22 us: extended(): lax.ppermute(tail, axis, [(i, (i + 1) % count) for i in range(ends)])]
    pallas_call x0 -> x1, Pallas kernels: none -> 21.5 us  [local(): pl.pallas_call(functools.partial(kernel, groups, layers, n), out_shape=[j...]
    all_to_all x4 -> x0, starting transfers between devices: 18.8 us -> none  [the longest x1 7.08 us: local(): lax.all_to_all(to_lines(cotangent), 'gy', split_axis=2, concat_axis=1, ti...]
    all_to_all x4 -> x0, waiting for transfers between devices: 14.9 us -> none  [the longest x1 7.92 us: local(): lax.all_to_all(line_solve(lax.all_to_all(to_lines(cotangent), 'gy', split...]
    ppermute x12 -> x0, waiting for transfers between devices: 8.25 us -> none  [the longest x6 5.71 us: extended(): lax.ppermute(head, axis, [((i + 1) % count, i) for i in range(ends)])]
    dot_general x5 -> x0, matrix products: 6.11 us -> none  [the longest x2 3 us: line_solve(): jnp.einsum('ky,cyl->ckl', sine_table, flat, precision=lax.Precision.HIGHEST)]
    mul x7 -> x0, other arithmetic: 4.62 us -> none  [the longest x2 1.99 us: slope_x(): return 0.5 * (padded[..., 2:] - padded[..., :-2])]
    slice x5 -> x0, other arithmetic: 3.55 us -> none  [the longest x4 3.27 us: extended(): lax.slice_in_dim(cells, cells.shape[dim] - width, cells.shape[dim], axis=...]
  transfers between devices with their start and end apart: 16 -> 0, of which waited for: 6 -> 0; matrix products, arithmetic and copies ran while one was open for 23% -> 0% of each run, Pallas kernels for 0% -> 0%
where the time goes in v1:
time: 29.9 us; the launch traced here: 29.5 us
  Pallas kernels  21.5 us (72%)
  local copies, waits for them, and re-layouts  7.32 us (24%)
  between operations  0.65 us (2%)
    pallas_call x1, Pallas kernels, local(): pl.pallas_call(functools.partial(kernel, groups, layers, n), out_shape=[j...  21.5 us
    unnamed x14, local copies, waits for them, and re-layouts  7.32 us

profile of v1, /device:TPU:0, one launch (start us, length us, event | category | flops | bytes accessed | tf_op | source)
XLA Modules:
  0.0 29.5 jit_solution(8382809312686495741)
XLA Ops:
  0.6 0.0 copy-start.5
  0.6 0.6 %copy-done.5 = f32[8]{0:T(128)S(1)} copy-done((f32[8]{0:T(128)S(1)}, f32[8]{0:T(128)}, u32[]{:S(2)}) %copy-start.5) | copy-done | bytes 56
  1.3 0.0 copy-start
  1.3 1.1 %copy-done = f32[3,24,8,256]{3,2,1,0:T(8,128)S(1)} copy-done((f32[3,24,8,256]{3,2,1,0:T(8,128)S(1)}, f32[3,24,8,256]{3,2,1,0:T(8,128)}, u32[]{:S(2)}) %copy-start) | copy-done | bytes 589848
  2.4 0.0 copy-start.1
  2.4 1.1 %copy-done.1 = f32[3,24,8,256]{3,2,1,0:T(8,128)S(1)} copy-done((f32[3,24,8,256]{3,2,1,0:T(8,128)S(1)}, f32[3,24,8,256]{3,2,1,0:T(8,128)}, u32[]{:S(2)}) %copy-start.1) | copy-done | bytes 589848
  3.4 0.0 copy-start.2
  3.4 1.1 %copy-done.2 = f32[3,24,8,256]{3,2,1,0:T(8,128)S(1)} copy-done((f32[3,24,8,256]{3,2,1,0:T(8,128)S(1)}, f32[3,24,8,256]{3,2,1,0:T(8,128)}, u32[]{:S(2)}) %copy-start.2) | copy-done | bytes 589848
  4.5 0.0 copy-start.3
  4.5 0.9 %copy-done.3 = f32[24,8,256]{2,1,0:T(8,128)S(1)} copy-done((f32[24,8,256]{2,1,0:T(8,128)S(1)}, f32[24,8,256]{2,1,0:T(8,128)}, u32[]{:S(2)}) %copy-start.3) | copy-done | bytes 196632
  5.4 0.0 copy-start.4
  5.4 0.9 %copy-done.4 = s32[24,8,256]{2,1,0:T(8,128)S(1)} copy-done((s32[24,8,256]{2,1,0:T(8,128)S(1)}, s32[24,8,256]{2,1,0:T(8,128)}, u32[]{:S(2)}) %copy-start.4) | copy-done | bytes 196632
  6.3 21.5 %shard_map.77 = (f32[3,24,8,256]{3,2,1,0:T(8,128)S(1)}, f32[3,24,8,256]{3,2,1,0:T(8,128)S(1)}) custom-call(f32[3,24,8,256]{3,2,1,0:T(8,128)S(1)} %copy-done, f32[3,24,8,256]{3,2,1,0:T(8,128)S(1)} %copy-done.1, f32[24,8,256]{2,1,0:T(8,128)S(1)} %copy-done.3, s32[24,8,256]{2,1,0:T(8,128)S(1)} %copy-done.4, f32[1,8]{1,0:T(1,128)S(1)} %bitcast.1, ...), custom_call_target="tpu_custom_call" | custom-call | tf_op jit(solution)/shard_map/pallas_call | solution.py:434
  27.9 0.8 %copy.10 = f32[3,24,8,256]{3,2,1,0:T(8,128)} copy(f32[3,24,8,256]{3,2,1,0:T(8,128)S(1)} %get-tuple-element.4) | data formatting | bytes 1179648
  28.7 0.8 %copy.11 = f32[3,24,8,256]{3,2,1,0:T(8,128)} copy(f32[3,24,8,256]{3,2,1,0:T(8,128)S(1)} %get-tuple-element.5) | data formatting | bytes 1179648
Async XLA Ops:
  0.6 0.7 %copy-start.5 = (f32[8]{0:T(128)S(1)}, f32[8]{0:T(128)}, u32[]{:S(2)}) copy-start(f32[8]{0:T(128)} %param.10) | copy-start | bytes 100
  1.3 1.1 %copy-start = (f32[3,24,8,256]{3,2,1,0:T(8,128)S(1)}, f32[3,24,8,256]{3,2,1,0:T(8,128)}, u32[]{:S(2)}) copy-start(f32[3,24,8,256]{3,2,1,0:T(8,128)} %mag.1) | copy-start | bytes 1769476
  2.4 1.1 %copy-start.1 = (f32[3,24,8,256]{3,2,1,0:T(8,128)S(1)}, f32[3,24,8,256]{3,2,1,0:T(8,128)}, u32[]{:S(2)}) copy-start(f32[3,24,8,256]{3,2,1,0:T(8,128)} %vel.1) | copy-start | bytes 1769476
  3.4 1.1 %copy-start.2 = (f32[3,24,8,256]{3,2,1,0:T(8,128)S(1)}, f32[3,24,8,256]{3,2,1,0:T(8,128)}, u32[]{:S(2)}) copy-start(f32[3,24,8,256]{3,2,1,0:T(8,128)} %cot.1) | copy-start | bytes 1769476
  4.5 0.9 %copy-start.3 = (f32[24,8,256]{2,1,0:T(8,128)S(1)}, f32[24,8,256]{2,1,0:T(8,128)}, u32[]{:S(2)}) copy-start(f32[24,8,256]{2,1,0:T(8,128)} %dif.1) | copy-start | bytes 589828
  5.4 0.9 %copy-start.4 = (s32[24,8,256]{2,1,0:T(8,128)S(1)}, s32[24,8,256]{2,1,0:T(8,128)}, u32[]{:S(2)}) copy-start(s32[24,8,256]{2,1,0:T(8,128)} %mat.1) | copy-start | bytes 589828

commit v2 on v1

--- a/solution.py
+++ b/solution.py
@@ -14,15 +14,17 @@
 
 
 def kernel(
-    groups, layers, n, mag, vel, dif, mat, rate, cot, new_out, adj_out,
-    bE, gE, wE, hE, v, eta, iron, adj, new, zs, zr, ends, m_tab, inv_tab, al_tab, s_tab, den_tab,
-    load_sem, out_sem, ys_sem, yr_sem, zs_sem, zr_sem, gs_sem, gr_sem,
+    groups, layers, n, mag, vel, dif, mat, rate, cot, new, adj,
+    bE, gE, wE, hE, v, eta, iron, rate_row, zs, zr, ends, m_tab, inv_tab, al_tab, s_tab, den_tab,
+    load_sem, ys_sem, yr_sem, zs_sem, zr_sem, gs_sem, gr_sem,
 ):
     me = lax.axis_index("gy")
     lay = lax.axis_index("gz")
     nx = bE.shape[-1]
     nz = bE.shape[-2]
 
+    rate_load = pltpu.make_async_copy(rate, rate_row, load_sem.at[5])
+    rate_load.start()
     loads = [
         pltpu.make_async_copy(mag, bE.at[:, pl.ds(1, n)], load_sem.at[0]),
         pltpu.make_async_copy(cot, wE.at[:, pl.ds(1, n)], load_sem.at[1]),
@@ -74,7 +76,8 @@
     square = (
         lax.broadcasted_iota(jnp.int32, (nz, nz), 0) == lax.broadcasted_iota(jnp.int32, (nz, nz), 1)
     )
-    r = jnp.sum(jnp.where(square, jnp.broadcast_to(rate[...], (nz, nz)), 0.0), axis=1, keepdims=True)
+    rate_load.wait()
+    r = jnp.sum(jnp.where(square, jnp.broadcast_to(rate_row[...], (nz, nz)), 0.0), axis=1, keepdims=True)
     r = jnp.broadcast_to(r, (nz, nx))
 
     def pivot(k, p):
@@ -400,8 +403,6 @@
             new[c, y] = new[c, y] + near * gE[c, 0] + far * gE[c, n + 1]
 
     each_row(finish)
-    new_copy = pltpu.make_async_copy(new, new_out, out_sem.at[0])
-    new_copy.start()
 
     recv(hE, 3)
 
@@ -411,8 +412,6 @@
             adj[c, y] = adj[c, y] - step_size * turn[c]
 
     each_row(finish_adjoint)
-    adj_copy = pltpu.make_async_copy(adj, adj_out, out_sem.at[1])
-    adj_copy.start()
     done_sending(bE, 0)
     done_sending(gE, 1)
     done_sending(None, 2)
@@ -420,8 +419,17 @@
     for slot in range(2):
         for copy in gather(slot):
             copy.wait_send()
-    new_copy.wait()
-    adj_copy.wait()
+
+
+def hand_over(new, adj, new_out, adj_out, sem):
+    copies = [
+        pltpu.make_async_copy(new, new_out, sem.at[0]),
+        pltpu.make_async_copy(adj, adj_out, sem.at[1]),
+    ]
+    for copy in copies:
+        copy.start()
+    for copy in copies:
+        copy.wait()
 
 
 def local(groups, layers, magnetic, velocity, diffusivity, material, plane_rate, cotangent):
@@ -431,11 +439,15 @@
     f32 = jnp.float32
     anywhere = pl.BlockSpec(memory_space=pl.ANY)
     inside = pl.BlockSpec(memory_space=pltpu.VMEM)
-    return tuple(pl.pallas_call(
+    args = [
+        pltpu.with_memory_space_constraint(array, pltpu.HBM)
+        for array in (magnetic, velocity, diffusivity, material, plane_rate.reshape(1, nz), cotangent)
+    ]
+    new, adj = pl.pallas_call(
         functools.partial(kernel, groups, layers, n),
         out_shape=[jax.ShapeDtypeStruct(block, f32)] * 2,
-        in_specs=[anywhere] * 4 + [inside] + [anywhere],
-        out_specs=[anywhere] * 2,
+        in_specs=[anywhere] * 6,
+        out_specs=[inside] * 2,
         scratch_shapes=[
             pltpu.VMEM(rimmed, f32),
             pltpu.VMEM(rimmed, f32),
@@ -444,8 +456,7 @@
             pltpu.VMEM(block, f32),
             pltpu.VMEM((n, nz, nx), f32),
             pltpu.VMEM((n, nz, nx), jnp.int32),
-            pltpu.VMEM(block, f32),
-            pltpu.VMEM(block, f32),
+            pltpu.VMEM((1, nz), f32),
             pltpu.VMEM((4, 2, 2, n, nx), f32),
             pltpu.VMEM((4, 2, 2, n, nx), f32),
             pltpu.VMEM((2, groups, 2, 3, nz, nx), f32),
@@ -454,8 +465,7 @@
             pltpu.VMEM((n, nz, nx), f32),
             pltpu.VMEM((groups, nz, nx), f32),
             pltpu.VMEM((groups, nz, nx), f32),
-            pltpu.SemaphoreType.DMA((5,)),
-            pltpu.SemaphoreType.DMA((2,)),
+            pltpu.SemaphoreType.DMA((6,)),
             pltpu.SemaphoreType.DMA((4, 2, 2)),
             pltpu.SemaphoreType.DMA((4, 2, 2)),
             pltpu.SemaphoreType.DMA((4, 2)),
@@ -466,7 +476,15 @@
         compiler_params=pltpu.CompilerParams(
             collective_id=0, has_side_effects=True, vmem_limit_bytes=24 * 2**20
         ),
-    )(magnetic, velocity, diffusivity, material, plane_rate.reshape(1, nz), cotangent))
+    )(*args)
+    return tuple(pl.pallas_call(
+        hand_over,
+        out_shape=[jax.ShapeDtypeStruct(block, f32)] * 2,
+        in_specs=[anywhere] * 2,
+        out_specs=[anywhere] * 2,
+        scratch_shapes=[pltpu.SemaphoreType.DMA((2,))],
+        compiler_params=pltpu.CompilerParams(vmem_limit_bytes=2**20),
+    )(new, adj))
 
 
 def solution(mesh):

time: 29.9 us -> 22.5 us (0.75)
  local copies, waits for them, and re-layouts: 7.32 us -> 0 us
    unnamed x14 -> x0, local copies, waits for them, and re-layouts: 7.32 us -> none
    pallas_call x0 -> x1, Pallas kernels: none -> 1.03 us  [local(): pl.pallas_call(hand_over, out_shape=[jax.ShapeDtypeStruct(block, f32)] *...]
    pallas_call x1, Pallas kernels: 21.5 us -> 20.7 us  [local(): pl.pallas_call(functools.partial(kernel, groups, layers, n), out_shape=[j...]
where the time goes in v2:
time: 22.5 us; the launch traced here: 22.4 us
  Pallas kernels  21.7 us (96%)
  between operations  0.64 us (3%)
    pallas_call x1, Pallas kernels, local(): pl.pallas_call(functools.partial(kernel, groups, layers, n), out_shape=[j...  20.7 us
    pallas_call x1, Pallas kernels, local(): pl.pallas_call(hand_over, out_shape=[jax.ShapeDtypeStruct(block, f32)] *...  1.03 us

profile of v2, /device:TPU:0, one launch (start us, length us, event | category | flops | bytes accessed | tf_op | source)
XLA Modules:
  0.0 22.4 jit_solution(11674303039315675048)
XLA Ops:
  0.6 20.7 %shard_map.77 = (f32[3,24,8,256]{3,2,1,0:T(8,128)S(1)}, f32[3,24,8,256]{3,2,1,0:T(8,128)S(1)}) custom-call(f32[3,24,8,256]{3,2,1,0:T(8,128)} %mag.1, f32[3,24,8,256]{3,2,1,0:T(8,128)} %vel.1, f32[24,8,256]{2,1,0:T(8,128)} %dif.1, s32[24,8,256]{2,1,0:T(8,128)} %mat.1, f32[1,8]{1,0:T(1,128)} %bitcast.1, f32[3,24,8,256]{3,2,1,0:T(8,128)} %cot.1), custom_call_target="tpu_custom_call" | custom-call | tf_op jit(solution)/shard_map/pallas_call | solution.py:446
  21.3 1.0 %shard_map.78 = (f32[3,24,8,256]{3,2,1,0:T(8,128)}, f32[3,24,8,256]{3,2,1,0:T(8,128)}) custom-call(f32[3,24,8,256]{3,2,1,0:T(8,128)S(1)} %get-tuple-element.4.new, f32[3,24,8,256]{3,2,1,0:T(8,128)S(1)} %get-tuple-element.5.adj), custom_call_target="tpu_custom_call" | custom-call | tf_op jit(solution)/shard_map/pallas_call | solution.py:480

commit v3 on v2

--- a/solution.py
+++ b/solution.py
@@ -15,13 +15,14 @@
 
 def kernel(
     groups, layers, n, mag, vel, dif, mat, rate, cot, new, adj,
-    bE, gE, wE, hE, v, eta, iron, rate_row, zs, zr, ends, m_tab, inv_tab, al_tab, s_tab, den_tab,
+    bE, gE, wE, hE, v, eta, iron, rate_row, zs, zr, ends, sums, m_tab, inv_tab, al_tab, s_tab, den_tab, mix,
     load_sem, ys_sem, yr_sem, zs_sem, zr_sem, gs_sem, gr_sem,
 ):
     me = lax.axis_index("gy")
     lay = lax.axis_index("gz")
     nx = bE.shape[-1]
     nz = bE.shape[-2]
+    parts, depth = zs.shape[2], zs.shape[4]
 
     rate_load = pltpu.make_async_copy(rate, rate_row, load_sem.at[5])
     rate_load.start()
@@ -104,6 +105,17 @@
         return aa + cc * s * den
 
     lax.fori_loop(0, groups, reach, jnp.zeros((nz, nx), jnp.float32))
+    s_low, s_high = s_tab[me], s_tab[groups - 1 - me]
+    left_gap, right_gap = 1.0 - s_low * aa, 1.0 - s_high * aa
+    det = 1.0 / (left_gap * right_gap - s_low * s_high * cc * cc)
+    mix[0] = right_gap * det
+    mix[1] = s_low * cc * det
+    mix[2] = left_gap * det
+    mix[3] = s_high * cc * det
+    mix[4] = den_tab[me] * s_low
+    mix[5] = den_tab[groups - 1 - me] * s_high
+    mix[6] = s_low
+    mix[7] = s_high
 
     def local_solve(field, offset, slot):
         def down(k, held):
@@ -126,18 +138,20 @@
 
         lax.fori_loop(0, n, up, (zero, zero, zero), unroll=True)
         for c in range(3):
-            ends[slot, me, 0, c] = field[c, offset]
-            ends[slot, me, 1, c] = field[c, offset + n - 1]
+            first, last = field[c, offset], field[c, offset + n - 1]
+            sums[slot, 0, c] = last + mix[4] * first
+            sums[slot, 1, c] = first + mix[5] * last
 
     def gather(slot):
-        return [
-            pltpu.make_async_remote_copy(
-                src_ref=ends.at[slot, me], dst_ref=ends.at[slot, me],
+        copies = []
+        for k in range(1, groups):
+            partner = lax.rem(me + k, groups)
+            copies.append(pltpu.make_async_remote_copy(
+                src_ref=sums.at[slot, (partner < me).astype(jnp.int32)], dst_ref=ends.at[slot, me],
                 send_sem=gs_sem.at[slot, k], recv_sem=gr_sem.at[slot, k],
-                device_id={"gy": lax.rem(me + k, groups), "gz": lay}, device_id_type=MESH,
-            )
-            for k in range(1, groups)
-        ]
+                device_id={"gy": partner, "gz": lay}, device_id_type=MESH,
+            ))
+        return copies
 
     def gather_wait(slot):
         for k in range(1, groups):
@@ -148,38 +162,25 @@
                 device_id={"gy": src, "gz": lay}, device_id_type=MESH,
             ).wait_recv()
 
-    def interface(slot):
+    def interface(slot, field, offset):
         zero = jnp.zeros((nz, nx), jnp.float32)
 
         def sweep(k, held):
-            low, high, s_low, s_high = held
-            s, den = s_tab[k], den_tab[k]
-            take_low = k < me
+            low, high = held
+            den = den_tab[k]
             far = groups - 1 - k
-            take_high = far > me
-            low = tuple(
-                jnp.where(take_low, ends[slot, k, 1, c] + den * (low[c] + s * ends[slot, k, 0, c]), low[c])
-                for c in range(3)
-            )
-            high = tuple(
-                jnp.where(take_high, ends[slot, far, 0, c] + den * (high[c] + s * ends[slot, far, 1, c]), high[c])
-                for c in range(3)
-            )
-            after = s_tab[k + 1]
-            s_low = jnp.where(take_low, after, s_low)
-            s_high = jnp.where(take_high, after, s_high)
-            return low, high, s_low, s_high
+            low = tuple(jnp.where(k < me, ends[slot, k, c] + den * low[c], low[c]) for c in range(3))
+            high = tuple(jnp.where(far > me, ends[slot, far, c] + den * high[c], high[c]) for c in range(3))
+            return low, high
 
         zeros = (zero, zero, zero)
-        low, high, s_low, s_high = lax.fori_loop(0, groups - 1, sweep, (zeros, zeros, zero, zero))
-        left_gap, right_gap = 1.0 - s_low * aa, 1.0 - s_high * aa
-        det = 1.0 / (left_gap * right_gap - s_low * s_high * cc * cc)
+        low, high = lax.fori_loop(0, groups - 1, sweep, (zeros, zeros), unroll=groups <= 8)
         lefts, rights = [], []
         for c in range(3):
-            x = low[c] + s_low * ends[slot, me, 0, c]
-            y = high[c] + s_high * ends[slot, me, 1, c]
-            lefts.append((right_gap * x + s_low * cc * y) * det)
-            rights.append((left_gap * y + s_high * cc * x) * det)
+            x = low[c] + mix[6] * field[c, offset]
+            y = high[c] + mix[7] * field[c, offset + n - 1]
+            lefts.append(mix[0] * x + mix[1] * y)
+            rights.append(mix[2] * y + mix[3] * x)
         return lefts, rights
 
     def y_copies(field, ex):
@@ -195,32 +196,31 @@
                 device_id={"gy": jnp.minimum(me + 1, groups - 1), "gz": lay}, device_id_type=MESH))
         return lefts, rights
 
-    def z_copies(ex):
+    def z_copies(ex, part):
         low = pltpu.make_async_remote_copy(
-            src_ref=zs.at[ex, 0], dst_ref=zr.at[ex, 1],
-            send_sem=zs_sem.at[ex, 0], recv_sem=zr_sem.at[ex, 0],
+            src_ref=zs.at[ex, 0, part], dst_ref=zr.at[ex, 1, part],
+            send_sem=zs_sem.at[ex, 0, part], recv_sem=zr_sem.at[ex, 0, part],
             device_id={"gy": me, "gz": jnp.maximum(lay - 1, 0)}, device_id_type=MESH)
         high = pltpu.make_async_remote_copy(
-            src_ref=zs.at[ex, 1], dst_ref=zr.at[ex, 0],
-            send_sem=zs_sem.at[ex, 1], recv_sem=zr_sem.at[ex, 1],
+            src_ref=zs.at[ex, 1, part], dst_ref=zr.at[ex, 0, part],
+            send_sem=zs_sem.at[ex, 1, part], recv_sem=zr_sem.at[ex, 1, part],
             device_id={"gy": me, "gz": jnp.minimum(lay + 1, layers - 1)}, device_id_type=MESH)
         return low, high
 
-    def send_y(field, ex):
-        lefts, rights = y_copies(field, ex)
-
+    def send_left(field, ex):
         @pl.when(has_left)
         def _():
-            for copy in lefts:
+            for copy in y_copies(field, ex)[0]:
                 copy.start()
 
+    def send_right(field, ex):
         @pl.when(has_right)
         def _():
-            for copy in rights:
+            for copy in y_copies(field, ex)[1]:
                 copy.start()
 
-    def send_z(ex):
-        low, high = z_copies(ex)
+    def send_z(ex, part):
+        low, high = z_copies(ex, part)
 
         @pl.when(has_low)
         def _():
@@ -230,20 +230,20 @@
         def _():
             high.start()
 
-    def recv(field, ex):
-        low, high = z_copies(ex)
-        if field is not None:
-            lefts, rights = y_copies(field, ex)
-
-            @pl.when(has_right)
-            def _():
-                for copy in lefts:
-                    copy.wait_recv()
-
-            @pl.when(has_left)
-            def _():
-                for copy in rights:
-                    copy.wait_recv()
+    def recv_left(field, ex):
+        @pl.when(has_left)
+        def _():
+            for copy in y_copies(field, ex)[1]:
+                copy.wait_recv()
+
+    def recv_right(field, ex):
+        @pl.when(has_right)
+        def _():
+            for copy in y_copies(field, ex)[0]:
+                copy.wait_recv()
+
+    def recv_z(ex, part):
+        low, high = z_copies(ex, part)
 
         @pl.when(has_high)
         def _():
@@ -254,7 +254,6 @@
             high.wait_recv()
 
     def done_sending(field, ex):
-        low, high = z_copies(ex)
         if field is not None:
             lefts, rights = y_copies(field, ex)
 
@@ -268,55 +267,63 @@
                 for copy in rights:
                     copy.wait_send()
 
-        @pl.when(has_low)
-        def _():
-            low.wait_send()
-
-        @pl.when(has_high)
-        def _():
-            high.wait_send()
-
-    def stage(ex, y, rows):
-        for i in range(2):
-            zs[ex, 0, i, pl.ds(y, 1), :] = rows[i][0:1]
-            zs[ex, 1, i, pl.ds(y, 1), :] = rows[i][nz - 1:nz]
+        for part in range(parts):
+            low, high = z_copies(ex, part)
+
+            @pl.when(has_low)
+            def _():
+                low.wait_send()
+
+            @pl.when(has_high)
+            def _():
+                high.wait_send()
+
+    def stage(ex, part, i, rows):
+        for c in range(2):
+            zs[ex, 0, part, c, pl.ds(i, 1), :] = rows[c][0:1]
+            zs[ex, 1, part, c, pl.ds(i, 1), :] = rows[c][nz - 1:nz]
 
     def slope_x(f):
         ahead = jnp.where(lane == nx - 1, 0.0, pltpu.roll(f, nx - 1, 1))
         behind = jnp.where(lane == 0, 0.0, pltpu.roll(f, 1, 1))
         return 0.5 * (ahead - behind)
 
-    def slope_z(f, ex, i, y):
-        below = jnp.broadcast_to(zr[ex, 0, i, pl.ds(y, 1), :], (nz, nx))
-        above = jnp.broadcast_to(zr[ex, 1, i, pl.ds(y, 1), :], (nz, nx))
+    def slope_z(f, ex, c, part, i):
+        below = jnp.broadcast_to(zr[ex, 0, part, c, pl.ds(i, 1), :], (nz, nx))
+        above = jnp.broadcast_to(zr[ex, 1, part, c, pl.ds(i, 1), :], (nz, nx))
         ahead = jnp.where(sub == nz - 1, above, pltpu.roll(f, nz - 1, 0))
         behind = jnp.where(sub == 0, below, pltpu.roll(f, 1, 0))
         return 0.5 * (ahead - behind)
 
-    def curl(field, ex, y):
+    def curl(field, ex, part, i):
+        y = part * depth + i
         f = [field[c, y + 1] for c in range(3)]
         dy_x = 0.5 * (field[0, y + 2] - field[0, y])
         dy_z = 0.5 * (field[2, y + 2] - field[2, y])
         return (
-            dy_z - slope_z(f[1], ex, 1, y),
-            slope_z(f[0], ex, 0, y) - slope_x(f[2]),
+            dy_z - slope_z(f[1], ex, 1, part, i),
+            slope_z(f[0], ex, 0, part, i) - slope_x(f[2]),
             slope_x(f[1]) - dy_x,
         ), f
 
-    def each_row(body, unroll=2):
+    def each_row(body, part, unroll=2):
         def some(step, carry):
             for u in range(unroll):
-                body(step * unroll + u)
+                body(part, step * unroll + u)
             return carry
 
-        lax.fori_loop(0, n // unroll, some, 0)
+        lax.fori_loop(0, depth // unroll, some, 0)
 
     loads[0].wait()
-    each_row(lambda y: stage(0, y, (bE[0, y + 1], bE[1, y + 1])), 4)
+    for part in range(parts):
+        each_row(lambda p, i: stage(0, p, i, (bE[0, p * depth + i + 1], bE[1, p * depth + i + 1])), part, 4)
     count = groups - 1 + has_low.astype(jnp.int32) + has_high.astype(jnp.int32)
     pl.semaphore_wait(barrier, count)
-    send_y(bE, 0)
-    send_z(0)
+    send_z(0, 0)
+    send_left(bE, 0)
+    send_right(bE, 0)
+    for part in range(1, parts):
+        send_z(0, part)
 
     loads[1].wait()
     local_solve(wE, 1, 0)
@@ -325,12 +332,12 @@
 
     for load in loads[2:]:
         load.wait()
-    recv(bE, 0)
-
-    def argument(y):
+
+    def argument(part, i):
+        y = part * depth + i
         spread = eta[y] * (1.0 - (1.0 - iron_factor) * iron[y].astype(jnp.float32))
         eta[y] = spread
-        turn, b = curl(bE, 0, y)
+        turn, b = curl(bE, 0, part, i)
         s = [v[c, y] for c in range(3)]
         rows = (
             s[1] * b[2] - s[2] * b[1] - spread * turn[0],
@@ -339,44 +346,56 @@
         )
         for c in range(3):
             gE[c, y + 1] = rows[c]
-        stage(1, y, rows)
-
-    each_row(argument)
-    send_y(gE, 1)
-    send_z(1)
+        stage(1, part, i, rows)
+
+    recv_left(bE, 0)
+    for part in range(parts):
+        if part == parts - 1:
+            recv_right(bE, 0)
+        recv_z(0, part)
+        each_row(argument, part)
+        send_z(1, part)
+        if part == 0:
+            send_left(gE, 1)
+    send_right(gE, 1)
 
     gather_wait(0)
-    lefts, rights = interface(0)
+    lefts, rights = interface(0, wE, 1)
     for c in range(3):
         wE[c, 0] = lefts[c]
         wE[c, n + 1] = rights[c]
 
-    def relax(y):
+    def relax(part, i):
+        y = part * depth + i
         near, far = al_tab[y], al_tab[n - 1 - y]
         rows = [wE[c, y + 1] + near * wE[c, 0] + far * wE[c, n + 1] for c in range(3)]
         for c in range(3):
             wE[c, y + 1] = rows[c]
-        stage(2, y, rows)
-
-    each_row(relax)
-    send_z(2)
-
-    recv(gE, 1)
-
-    def advance(y):
-        turn, _ = curl(gE, 1, y)
+        stage(2, part, i, rows)
+
+    for part in range(parts):
+        each_row(relax, part)
+        send_z(2, part)
+
+    def advance(part, i):
+        y = part * depth + i
+        turn, _ = curl(gE, 1, part, i)
         for c in range(3):
             new[c, y] = bE[c, y + 1] + step_size * turn[c]
 
-    each_row(advance)
+    recv_left(gE, 1)
+    for part in range(parts):
+        if part == parts - 1:
+            recv_right(gE, 1)
+        recv_z(1, part)
+        each_row(advance, part)
     local_solve(new, 0, 1)
     for copy in gather(1):
         copy.start()
 
-    recv(None, 2)
-
-    def pull(y):
-        turn, w = curl(wE, 2, y)
+    def pull(part, i):
+        y = part * depth + i
+        turn, w = curl(wE, 2, part, i)
         s = [v[c, y] for c in range(3)]
         spread = eta[y]
         adj[0, y] = w[0] + step_size * (turn[1] * s[2] - turn[2] * s[1])
@@ -385,33 +404,43 @@
         rows = [spread * turn[c] for c in range(3)]
         for c in range(3):
             hE[c, y + 1] = rows[c]
-        stage(3, y, rows)
-
-    each_row(pull)
-    send_y(hE, 3)
-    send_z(3)
+        stage(3, part, i, rows)
+
+    for part in range(parts):
+        recv_z(2, part)
+        each_row(pull, part)
+        send_z(3, part)
+        if part == 0:
+            send_left(hE, 3)
+    send_right(hE, 3)
+
+    def finish_adjoint(part, i):
+        y = part * depth + i
+        turn, _ = curl(hE, 3, part, i)
+        for c in range(3):
+            adj[c, y] = adj[c, y] - step_size * turn[c]
+
+    def finish(part, i):
+        y = part * depth + i
+        near, far = al_tab[y], al_tab[n - 1 - y]
+        for c in range(3):
+            new[c, y] = new[c, y] + near * gE[c, 0] + far * gE[c, n + 1]
 
     gather_wait(1)
-    lefts, rights = interface(1)
+    lefts, rights = interface(1, new, 0)
     for c in range(3):
         gE[c, 0] = lefts[c]
         gE[c, n + 1] = rights[c]
-
-    def finish(y):
-        near, far = al_tab[y], al_tab[n - 1 - y]
-        for c in range(3):
-            new[c, y] = new[c, y] + near * gE[c, 0] + far * gE[c, n + 1]
-
-    each_row(finish)
-
-    recv(hE, 3)
-
-    def finish_adjoint(y):
-        turn, _ = curl(hE, 3, y)
-        for c in range(3):
-            adj[c, y] = adj[c, y] - step_size * turn[c]
-
-    each_row(finish_adjoint)
+    for part in range(parts):
+        each_row(finish, part)
+
+    recv_left(hE, 3)
+    for part in range(parts):
+        if part == parts - 1:
+            recv_right(hE, 3)
+        recv_z(3, part)
+        each_row(finish_adjoint, part)
+
     done_sending(bE, 0)
     done_sending(gE, 1)
     done_sending(None, 2)
@@ -434,6 +463,7 @@
 
 def local(groups, layers, magnetic, velocity, diffusivity, material, plane_rate, cotangent):
     _, n, nz, nx = magnetic.shape
+    depth = 8 if n % 8 == 0 else n
     block = (3, n, nz, nx)
     rimmed = (3, n + 2, nz, nx)
     f32 = jnp.float32
@@ -457,19 +487,21 @@
             pltpu.VMEM((n, nz, nx), f32),
             pltpu.VMEM((n, nz, nx), jnp.int32),
             pltpu.VMEM((1, nz), f32),
-            pltpu.VMEM((4, 2, 2, n, nx), f32),
-            pltpu.VMEM((4, 2, 2, n, nx), f32),
-            pltpu.VMEM((2, groups, 2, 3, nz, nx), f32),
+            pltpu.VMEM((4, 2, n // depth, 2, depth, nx), f32),
+            pltpu.VMEM((4, 2, n // depth, 2, depth, nx), f32),
+            pltpu.VMEM((2, groups, 3, nz, nx), f32),
+            pltpu.VMEM((2, 2, 3, nz, nx), f32),
             pltpu.VMEM((n, nz, nx), f32),
             pltpu.VMEM((n, nz, nx), f32),
             pltpu.VMEM((n, nz, nx), f32),
             pltpu.VMEM((groups, nz, nx), f32),
             pltpu.VMEM((groups, nz, nx), f32),
+            pltpu.VMEM((8, nz, nx), f32),
             pltpu.SemaphoreType.DMA((6,)),
             pltpu.SemaphoreType.DMA((4, 2, 2)),
             pltpu.SemaphoreType.DMA((4, 2, 2)),
-            pltpu.SemaphoreType.DMA((4, 2)),
-            pltpu.SemaphoreType.DMA((4, 2)),
+            pltpu.SemaphoreType.DMA((4, 2, n // depth)),
+            pltpu.SemaphoreType.DMA((4, 2, n // depth)),
             pltpu.SemaphoreType.DMA((2, groups)),
             pltpu.SemaphoreType.DMA((2, groups)),
         ],

time: 22.5 us -> 20.1 us (0.89)
  Pallas kernels: 21.7 us -> 19.3 us
    pallas_call x1, Pallas kernels: 20.7 us -> 18.3 us  [local(): pl.pallas_call(functools.partial(kernel, groups, layers, n), out_shape=[j...]
where the time goes in v3:
time: 20.1 us; the launch traced here: 20 us
  Pallas kernels  19.3 us (96%)
  between operations  0.64 us (3%)
    pallas_call x1, Pallas kernels, local(): pl.pallas_call(functools.partial(kernel, groups, layers, n), out_shape=[j...  18.3 us
    pallas_call x1, Pallas kernels, local(): pl.pallas_call(hand_over, out_shape=[jax.ShapeDtypeStruct(block, f32)] *...  1.03 us

profile of v3, /device:TPU:0, one launch (start us, length us, event | category | flops | bytes accessed | tf_op | source)
XLA Modules:
  0.0 20.0 jit_solution(8730983981540162329)
XLA Ops:
  0.6 18.3 %shard_map.77 = (f32[3,24,8,256]{3,2,1,0:T(8,128)S(1)}, f32[3,24,8,256]{3,2,1,0:T(8,128)S(1)}) custom-call(f32[3,24,8,256]{3,2,1,0:T(8,128)} %mag.1, f32[3,24,8,256]{3,2,1,0:T(8,128)} %vel.1, f32[24,8,256]{2,1,0:T(8,128)} %dif.1, s32[24,8,256]{2,1,0:T(8,128)} %mat.1, f32[1,8]{1,0:T(1,128)} %bitcast.1, f32[3,24,8,256]{3,2,1,0:T(8,128)} %cot.1), custom_call_target="tpu_custom_call" | custom-call | tf_op jit(solution)/shard_map/pallas_call | solution.py:476
  18.9 1.0 %shard_map.78 = (f32[3,24,8,256]{3,2,1,0:T(8,128)}, f32[3,24,8,256]{3,2,1,0:T(8,128)}) custom-call(f32[3,24,8,256]{3,2,1,0:T(8,128)S(1)} %get-tuple-element.4.new, f32[3,24,8,256]{3,2,1,0:T(8,128)S(1)} %get-tuple-element.5.adj), custom_call_target="tpu_custom_call" | custom-call | tf_op jit(solution)/shard_map/pallas_call | solution.py:512

commit v4 on v3

--- a/solution.py
+++ b/solution.py
@@ -73,7 +73,7 @@
         zr[:, 1] = jnp.zeros(zr.shape[:1] + zr.shape[2:], jnp.float32)
 
     sub = lax.broadcasted_iota(jnp.int32, (nz, nx), 0)
-    lane = lax.broadcasted_iota(jnp.int32, (nz, nx), 1)
+    lane = lax.broadcasted_iota(jnp.int32, (nz, 128), 1)
     square = (
         lax.broadcasted_iota(jnp.int32, (nz, nz), 0) == lax.broadcasted_iota(jnp.int32, (nz, nz), 1)
     )
@@ -284,29 +284,38 @@
             zs[ex, 1, part, c, pl.ds(i, 1), :] = rows[c][nz - 1:nz]
 
     def slope_x(f):
-        ahead = jnp.where(lane == nx - 1, 0.0, pltpu.roll(f, nx - 1, 1))
-        behind = jnp.where(lane == 0, 0.0, pltpu.roll(f, 1, 1))
-        return 0.5 * (ahead - behind)
+        width = lane.shape[1]
+        tiles = [f[:, at:at + width] for at in range(0, nx, width)]
+        ahead = [pltpu.roll(tile, width - 1, 1) for tile in tiles] + [jnp.zeros_like(tiles[0])]
+        behind = [jnp.zeros_like(tiles[0])] + [pltpu.roll(tile, 1, 1) for tile in tiles]
+        return jnp.concatenate(
+            [
+                jnp.where(lane == width - 1, ahead[t + 1], ahead[t])
+                - jnp.where(lane == 0, behind[t], behind[t + 1])
+                for t in range(len(tiles))
+            ],
+            axis=1,
+        )
 
     def slope_z(f, ex, c, part, i):
         below = jnp.broadcast_to(zr[ex, 0, part, c, pl.ds(i, 1), :], (nz, nx))
         above = jnp.broadcast_to(zr[ex, 1, part, c, pl.ds(i, 1), :], (nz, nx))
         ahead = jnp.where(sub == nz - 1, above, pltpu.roll(f, nz - 1, 0))
         behind = jnp.where(sub == 0, below, pltpu.roll(f, 1, 0))
-        return 0.5 * (ahead - behind)
+        return ahead - behind
 
     def curl(field, ex, part, i):
         y = part * depth + i
         f = [field[c, y + 1] for c in range(3)]
-        dy_x = 0.5 * (field[0, y + 2] - field[0, y])
-        dy_z = 0.5 * (field[2, y + 2] - field[2, y])
+        dy_x = field[0, y + 2] - field[0, y]
+        dy_z = field[2, y + 2] - field[2, y]
         return (
             dy_z - slope_z(f[1], ex, 1, part, i),
             slope_z(f[0], ex, 0, part, i) - slope_x(f[2]),
             slope_x(f[1]) - dy_x,
         ), f
 
-    def each_row(body, part, unroll=2):
+    def each_row(body, part, unroll=4):
         def some(step, carry):
             for u in range(unroll):
                 body(part, step * unroll + u)
@@ -335,7 +344,7 @@
 
     def argument(part, i):
         y = part * depth + i
-        spread = eta[y] * (1.0 - (1.0 - iron_factor) * iron[y].astype(jnp.float32))
+        spread = eta[y] * (0.5 - 0.5 * (1.0 - iron_factor) * iron[y].astype(jnp.float32))
         eta[y] = spread
         turn, b = curl(bE, 0, part, i)
         s = [v[c, y] for c in range(3)]
@@ -381,7 +390,7 @@
         y = part * depth + i
         turn, _ = curl(gE, 1, part, i)
         for c in range(3):
-            new[c, y] = bE[c, y + 1] + step_size * turn[c]
+            new[c, y] = bE[c, y + 1] + 0.5 * step_size * turn[c]
 
     recv_left(gE, 1)
     for part in range(parts):
@@ -398,9 +407,9 @@
         turn, w = curl(wE, 2, part, i)
         s = [v[c, y] for c in range(3)]
         spread = eta[y]
-        adj[0, y] = w[0] + step_size * (turn[1] * s[2] - turn[2] * s[1])
-        adj[1, y] = w[1] + step_size * (turn[2] * s[0] - turn[0] * s[2])
-        adj[2, y] = w[2] + step_size * (turn[0] * s[1] - turn[1] * s[0])
+        adj[0, y] = w[0] + 0.5 * step_size * (turn[1] * s[2] - turn[2] * s[1])
+        adj[1, y] = w[1] + 0.5 * step_size * (turn[2] * s[0] - turn[0] * s[2])
+        adj[2, y] = w[2] + 0.5 * step_size * (turn[0] * s[1] - turn[1] * s[0])
         rows = [spread * turn[c] for c in range(3)]
         for c in range(3):
             hE[c, y + 1] = rows[c]
@@ -418,7 +427,7 @@
         y = part * depth + i
         turn, _ = curl(hE, 3, part, i)
         for c in range(3):
-            adj[c, y] = adj[c, y] - step_size * turn[c]
+            adj[c, y] = adj[c, y] - 0.5 * step_size * turn[c]
 
     def finish(part, i):
         y = part * depth + i

time: 20.1 us -> 19 us (0.945)
  Pallas kernels: 19.3 us -> 18.2 us
    pallas_call x1, Pallas kernels: 18.3 us -> 17.2 us  [local(): pl.pallas_call(functools.partial(kernel, groups, layers, n), out_shape=[j...]
where the time goes in v4:
time: 19 us; the launch traced here: 18.9 us
  Pallas kernels  18.2 us (96%)
  between operations  0.64 us (3%)
    pallas_call x1, Pallas kernels, local(): pl.pallas_call(functools.partial(kernel, groups, layers, n), out_shape=[j...  17.2 us
    pallas_call x1, Pallas kernels, local(): pl.pallas_call(hand_over, out_shape=[jax.ShapeDtypeStruct(block, f32)] *...  1.03 us

profile of v4, /device:TPU:0, one launch (start us, length us, event | category | flops | bytes accessed | tf_op | source)
XLA Modules:
  0.0 18.9 jit_solution(3244423536251422751)
XLA Ops:
  0.6 17.2 %shard_map.77 = (f32[3,24,8,256]{3,2,1,0:T(8,128)S(1)}, f32[3,24,8,256]{3,2,1,0:T(8,128)S(1)}) custom-call(f32[3,24,8,256]{3,2,1,0:T(8,128)} %mag.1, f32[3,24,8,256]{3,2,1,0:T(8,128)} %vel.1, f32[24,8,256]{2,1,0:T(8,128)} %dif.1, s32[24,8,256]{2,1,0:T(8,128)} %mat.1, f32[1,8]{1,0:T(1,128)} %bitcast.1, f32[3,24,8,256]{3,2,1,0:T(8,128)} %cot.1), custom_call_target="tpu_custom_call" | custom-call | tf_op jit(solution)/shard_map/pallas_call | solution.py:485
  17.8 1.0 %shard_map.78 = (f32[3,24,8,256]{3,2,1,0:T(8,128)}, f32[3,24,8,256]{3,2,1,0:T(8,128)}) custom-call(f32[3,24,8,256]{3,2,1,0:T(8,128)S(1)} %get-tuple-element.4.new, f32[3,24,8,256]{3,2,1,0:T(8,128)S(1)} %get-tuple-element.5.adj), custom_call_target="tpu_custom_call" | custom-call | tf_op jit(solution)/shard_map/pallas_call | solution.py:521

commit v5 on v4

--- a/solution.py
+++ b/solution.py
@@ -127,6 +127,10 @@
 
         zero = jnp.zeros((nz, nx), jnp.float32)
         lax.fori_loop(0, n, down, (zero, zero, zero), unroll=True)
+        local_rise(field, offset, slot)
+
+    def local_rise(field, offset, slot):
+        zero = jnp.zeros((nz, nx), jnp.float32)
 
         def up(step, held):
             k = n - 1 - step
@@ -386,19 +390,31 @@
         each_row(relax, part)
         send_z(2, part)
 
-    def advance(part, i):
-        y = part * depth + i
-        turn, _ = curl(gE, 1, part, i)
-        for c in range(3):
-            new[c, y] = bE[c, y + 1] + 0.5 * step_size * turn[c]
+    def advance(part, i, above):
+        y = part * depth + i
+        turn, b = curl(gE, 1, part, i)
+        m = m_tab[jnp.maximum(y - 1, 0)]
+        rows = tuple(bE[c, y + 1] + 0.5 * step_size * turn[c] + m * above[c] for c in range(3))
+        for c in range(3):
+            new[c, y] = rows[c]
+        return rows
+
+    def advance_part(part, above):
+        def some(step, held):
+            for u in range(4):
+                held = advance(part, step * 4 + u, held)
+            return held
+
+        return lax.fori_loop(0, depth // 4, some, above)
 
     recv_left(gE, 1)
+    carried = (rim, rim, rim)
     for part in range(parts):
         if part == parts - 1:
             recv_right(gE, 1)
         recv_z(1, part)
-        each_row(advance, part)
-    local_solve(new, 0, 1)
+        carried = advance_part(part, carried)
+    local_rise(new, 0, 1)
     for copy in gather(1):
         copy.start()
 

time: 19 us -> 19 us (level)
  no operation moved by 1% of the time
where the time goes in v5:
time: 19 us; the launch traced here: 18.8 us
  Pallas kernels  18.2 us (96%)
  between operations  0.64 us (3%)
    pallas_call x1, Pallas kernels, local(): pl.pallas_call(functools.partial(kernel, groups, layers, n), out_shape=[j...  17.2 us
    pallas_call x1, Pallas kernels, local(): pl.pallas_call(hand_over, out_shape=[jax.ShapeDtypeStruct(block, f32)] *...  1.03 us

profile of v5, /device:TPU:0, one launch (start us, length us, event | category | flops | bytes accessed | tf_op | source)
XLA Modules:
  0.0 18.8 jit_solution(7433101638720045555)
XLA Ops:
  0.6 17.2 %shard_map.77 = (f32[3,24,8,256]{3,2,1,0:T(8,128)S(1)}, f32[3,24,8,256]{3,2,1,0:T(8,128)S(1)}) custom-call(f32[3,24,8,256]{3,2,1,0:T(8,128)} %mag.1, f32[3,24,8,256]{3,2,1,0:T(8,128)} %vel.1, f32[24,8,256]{2,1,0:T(8,128)} %dif.1, s32[24,8,256]{2,1,0:T(8,128)} %mat.1, f32[1,8]{1,0:T(1,128)} %bitcast.1, f32[3,24,8,256]{3,2,1,0:T(8,128)} %cot.1), custom_call_target="tpu_custom_call" | custom-call | tf_op jit(solution)/shard_map/pallas_call | solution.py:501
  17.8 1.0 %shard_map.78 = (f32[3,24,8,256]{3,2,1,0:T(8,128)}, f32[3,24,8,256]{3,2,1,0:T(8,128)}) custom-call(f32[3,24,8,256]{3,2,1,0:T(8,128)S(1)} %get-tuple-element.4.new, f32[3,24,8,256]{3,2,1,0:T(8,128)S(1)} %get-tuple-element.5.adj), custom_call_target="tpu_custom_call" | custom-call | tf_op jit(solution)/shard_map/pallas_call | solution.py:537
